TPU v7x, 32 devices: a whole 2x2x4 slice. The times are simulated.
32 devices in a mesh: wide: 8 (over z, core), narrow: 4 (over y, x).
Axes of the slice: x: 2, y: 2, z: 4, core: 2. Of those that a mesh axis runs over, the one named last changes fastest.
Arguments:
- tokens: bfloat16 [8192, 2048], P('wide'), may hold values from -4 to 4
- cotangent: bfloat16 [8192, 2048], P('wide'), may hold values from -4 to 4
- noise_emb: float32 [128, 2048], P('wide'), may hold values from -2.5 to 2.5
- offsets: int32 [8, 16], P('wide'), may hold values from 0 to 1024, as said below
- lengths: int32 [8, 16], P('wide'), may hold values from 0 to 1024, as said below
- group_ids: int32 [8, 16], P('wide'), may hold values from 0 to 2, as said below
- group_table: float32 [3, 2048], replicated, may hold values from -2.5 to 2.5
- w_qkv: bfloat16 [3, 2048, 2048], P(None, None, 'narrow'), may hold values from -0.125 to 0.125
- w_out: bfloat16 [2048, 2048], P('narrow'), may hold values from -0.5 to 0.5
- w_up: bfloat16 [2048, 8192], P(None, 'narrow'), may hold values from -0.125 to 0.125
- b_up: float32 [8192], P('narrow'), may hold values from -2.5 to 2.5
- w_down: bfloat16 [8192, 2048], P('narrow'), may hold values from -0.09375 to 0.09375
- w_mod: bfloat16 [2048, 6, 2048], P(None, None, 'narrow'), may hold values from -0.0625 to 0.0625
- b_mod: float32 [6, 2048], P(None, 'narrow'), may hold values from -1.5 to 1.5
Outputs:
- result: bfloat16 [8192, 2048], P('wide')
- grad_tokens: bfloat16 [8192, 2048], P('wide')
- grad_noise: float32 [128, 2048], P('wide')
- grad_group_table: float32 [3, 2048], P(None, 'wide')
- grad_w_qkv: float32 [3, 2048, 2048], P(None, 'wide', 'narrow')
- grad_w_out: float32 [2048, 2048], P('narrow', 'wide')
- grad_w_up: float32 [2048, 8192], P('wide', 'narrow')
- grad_b_up: float32 [8192], P(('narrow', 'wide'))
- grad_w_down: float32 [8192, 2048], P('narrow', 'wide')
- grad_w_mod: float32 [2048, 6, 2048], P('wide', None, 'narrow')
- grad_b_mod: float32 [6, 2048], P(None, ('narrow', 'wide'))
Inputs may be any that keep to these rules, and one draw needn't show every extreme that they name: `offsets`: each index of wide holds images of one length, 1024, 256 or 64 tokens, laid end to end from token 0 and filling its 1024 tokens: slot s starts at s times that length. Slots past the last image start at 1024. Every length occurs on some index of wide. `lengths`: the length of each image slot; 0 for slots past the last image of an index of wide. `group_ids`: 0 on indices of wide with images of 1024 tokens, 1 with 256, 2 with 64, for all slots of that index; every group occurs.
All inputs are finite; a program needn't handle non-finite values.
Results may differ from a plain program's by a relative error of at most 0.018.
Values may be sent and summed in bfloat16 or wider, within the bound.
No kernel may reach another device: no remote copies, remote signals or barrier semaphores. Data moves between devices by JAX's collectives and lax.ppermute only.
A program may use at most 320 MiB of HBM per device.

v0:
```python
import jax
import jax.numpy as jnp
from jax import lax
from jax.experimental import pallas as pl
from jax.experimental.pallas import tpu as pltpu
from jax.sharding import PartitionSpec as P

HEAD_DIM = 128
SPAN = 64
MASKED = -1e30

f32 = jnp.float32
half = jnp.bfloat16
highest = lax.Precision.HIGHEST
MIB = 1 << 20


def dot(left, right, dims):
    return lax.dot_general(left, right, (dims, ((), ())), preferred_element_type=f32)


def normalize(values):
    centred = values - jnp.mean(values, axis=-1, keepdims=True)
    recip = lax.rsqrt(jnp.mean(centred * centred, axis=-1, keepdims=True) + 1e-06)
    return (centred * recip, recip)


def norm_back(grad, normed, recip):
    first = jnp.mean(grad, axis=-1, keepdims=True)
    second = jnp.mean(grad * normed, axis=-1, keepdims=True)
    return recip * (grad - first - normed * second)


def spec(shape, index):
    return pl.BlockSpec(shape, index)


def fixed(shape):
    zeros = (0,) * len(shape)
    return pl.BlockSpec(shape, lambda *_: zeros)


def held(shape):
    zeros = (0,) * len(shape)
    return pl.BlockSpec(shape, lambda *_: zeros, pipeline_mode=pl.Buffered(1))


def in_hbm(array):
    return pltpu.with_memory_space_constraint(array, pltpu.HBM)


def params(mib):
    return pltpu.CompilerParams(vmem_limit_bytes=mib * MIB)


def cost(micros):
    return pl.CostEstimate(flops=int(micros * 1.15e+09), transcendentals=0, bytes_accessed=0)


def shaped(shape, kind):
    return jax.ShapeDtypeStruct(shape, kind)


def after(values, *others):
    return lax.optimization_barrier((values, *others))[0]


def hop(values, distance, size):
    return lax.ppermute(values, "narrow", [(i, i ^ distance) for i in range(size)])


def exchange(chunks, size):
    return [chunks[0]] + [hop(chunks[d], d, size) for d in range(1, len(chunks))]


def spread_near(shard, size):
    return [shard] + [hop(shard, d, size) for d in range(1, size if size != 4 else 3)]


def spread(near, size, *gates):
    if size != 4:
        return [[piece] for piece in near]
    one, two = near[1:]
    mid = one.shape[0] // 2
    two, one = after(two[:mid], *gates), after(one[mid:], *gates)
    return [[piece] for piece in near] + [[hop(two, 1, size), hop(one, 2, size)]]


def joined(pieces):
    return jnp.concatenate(pieces, axis=0) if len(pieces) > 1 else pieces[0]


def flat(lists):
    return [piece for pieces in lists for piece in pieces]


def collect_far(far, size):
    if size != 4:
        return []
    mid = far.shape[0] // 2
    return [hop(far[:mid], 2, size), hop(far[mid:], 1, size)]


def collect_near(chunks, size, via):
    if size != 4:
        return chunks[1:]
    _, one, two, _ = chunks
    mid = one.shape[0] // 2
    via_two, via_one = via
    one = joined([(one[:mid].astype(f32) + via_two.astype(f32)).astype(half), one[mid:]])
    two = joined([two[:mid], (two[mid:].astype(f32) + via_one.astype(f32)).astype(half)])
    return [one, two]


def collect(chunks, size, via):
    return exchange(chunks[:1] + collect_near(chunks, size, via), size)


def in_order(pieces, index, axis):
    return jnp.concatenate([lax.select_n(index ^ k, *pieces) for k in range(len(pieces))], axis=axis)


def settle_kernel(layout, order_ref, *refs):
    out_ref = refs[-1]
    for d, count in enumerate(layout):

        @pl.when(pl.program_id(0) == d)
        def _(pieces=refs[sum(layout[:d]) :][:count]):
            at = 0
            for piece in pieces:
                out_ref[at : at + piece.shape[0], :] = piece[...]
                at += piece.shape[0]


def settle(chunks, order):
    rows = sum(piece.shape[0] for piece in chunks[0])
    width = chunks[0][0].shape[1]
    return pl.pallas_call(
        lambda *refs: settle_kernel([len(pieces) for pieces in chunks], *refs),
        grid_spec=pltpu.PrefetchScalarGridSpec(
            num_scalar_prefetch=1,
            grid=(len(chunks),),
            in_specs=[held(piece.shape) for piece in flat(chunks)],
            out_specs=spec((rows, width), lambda i, o: (o[i], 0)),
        ),
        out_shape=pltpu.HBM((rows * len(chunks), width), chunks[0][0].dtype),
        compiler_params=params(16),
        cost_estimate=cost(20),
        name="settle",
    )(order, *flat(chunks))


def modes_kernel(silu_ref, w_ref, b_ref, out_ref):
    for g in range(w_ref.shape[0]):
        out_ref[g] = jnp.dot(silu_ref[...], w_ref[g], preferred_element_type=f32) + b_ref[g]


def modes_call(silu_low, w_mod, b_mod, first, count):
    slots, width = silu_low.shape
    local = w_mod.shape[2]
    there = lambda i: (first // 2 + i, 0, 0)
    return pl.pallas_call(
        modes_kernel,
        grid=(count // 2,),
        in_specs=[
            fixed((slots, width)),
            spec((2, width, local), there),
            spec((2, 1, local), there),
        ],
        out_specs=spec((2, slots, local), lambda i: (i, 0, 0)),
        out_shape=shaped((count, slots, local), f32),
        cost_estimate=cost(1.5 * count),
        compiler_params=params(24),
        name="modes",
    )(silu_low, in_hbm(w_mod), b_mod[:, None, :])


def silu_back_kernel(d_ref, w_ref, out_ref):
    part = dot(d_ref[0], w_ref[0], ((1,), (1,)))

    @pl.when(pl.program_id(0) == 0)
    def _():
        out_ref[...] = part

    @pl.when(pl.program_id(0) > 0)
    def _():
        out_ref[...] = out_ref[...] + part


def silu_back_call(d_modes, w_mod):
    groups, slots, local = d_modes.shape
    width = w_mod.shape[1]
    return pl.pallas_call(
        silu_back_kernel,
        grid=(groups,),
        in_specs=[
            spec((1, slots, local), lambda g: (g, 0, 0)),
            spec((1, width, local), lambda g: (g, 0, 0)),
        ],
        out_specs=fixed((slots, width)),
        out_shape=shaped((slots, width), f32),
        compiler_params=params(16),
        cost_estimate=cost(0),
        name="silu_back",
    )(d_modes, in_hbm(w_mod))


def row_of(ref, slot):
    return ref[0, pl.ds(slot, 1), :]


def mix_kernel(order_ref, slot_ref, tok_ref, shift_ref, scale_ref, out_ref):
    step = pl.program_id(0)
    spans = tok_ref.shape[0] // SPAN
    for i in range(spans):
        rows = slice(i * SPAN, (i + 1) * SPAN)
        slot = slot_ref[step * spans + i]
        normed, _ = normalize(tok_ref[rows, :].astype(f32))
        out_ref[rows, :] = (normed * (1.0 + row_of(scale_ref, slot)) + row_of(shift_ref, slot)).astype(half)


def gate_kernel(order_ref, slot_ref, grad_ref, gate_ref, out_ref):
    step = pl.program_id(0)
    spans = grad_ref.shape[0] // SPAN
    for i in range(spans):
        rows = slice(i * SPAN, (i + 1) * SPAN)
        gate = row_of(gate_ref, slot_ref[step * spans + i])
        out_ref[rows, :] = (grad_ref[rows, :].astype(f32) * gate).astype(half)


def mode_specs(modes, columns):
    _, count, width = modes.shape
    return [spec((1, count, width), lambda i, *_, column=column: (column, 0, 0)) for column in columns]


def by_chunk(kernel, name, order, slots, values, modes, columns):
    rows, width = values.shape
    chunk = rows // order.shape[0]
    return pl.pallas_call(
        kernel,
        grid_spec=pltpu.PrefetchScalarGridSpec(
            num_scalar_prefetch=2,
            grid=(order.shape[0],),
            in_specs=[spec((chunk, width), lambda i, o, s: (o[i], 0))] + mode_specs(modes, columns),
            out_specs=spec((chunk, width), lambda i, o, s: (i, 0)),
        ),
        out_shape=shaped((rows, width), half),
        compiler_params=params(24),
        cost_estimate=cost(5),
        name=name,
    )(order, slots, values, *([modes] * len(columns)))


def product_kernel(dims, scales, left_ref, right_ref, out_ref):
    total = dot(left_ref[...], right_ref[...].reshape(right_ref.shape[-2:]), dims)
    if scales is not None:
        total = total * jnp.where(pl.program_id(0) == 0, scales, 1.0)
    out_ref[...] = total.astype(half).reshape(out_ref.shape)


def product(left, right, dims, name, block=512, out=shaped, micros=4, columns=None, first=0, before=None, gate=None):
    free = 1 - dims[1][0]
    count = right.shape[free]
    rows = left.shape[1 - dims[0][0]]
    block = min(block, count)
    shape = (block, right.shape[1]) if free == 0 else (right.shape[0], block)
    index = (lambda j: (j, 0)) if free == 0 else (lambda j: (0, j))
    given = ([] if before is None else [before]) + ([] if gate is None else [gate])
    return pl.pallas_call(
        lambda left_ref, right_ref, *refs: product_kernel(dims, None, left_ref, right_ref, refs[-1]),
        grid=(count // block,),
        in_specs=[held(left.shape), spec(shape, index)] + [pl.BlockSpec(memory_space=pl.ANY)] * len(given),
        out_specs=spec((rows, block), lambda j: (0, first // block + j)),
        out_shape=out((rows, columns or count), half),
        input_output_aliases={} if before is None else {2: 0},
        compiler_params=params(28),
        cost_estimate=cost(micros),
        name=name,
    )(left, right, *given)


def project_call(mixed, w_qkv, factor):
    count, width, local = w_qkv.shape
    rows = mixed.shape[0]
    return pl.pallas_call(
        lambda *refs: product_kernel(((1,), (0,)), factor, *refs),
        grid=(count,),
        in_specs=[held(mixed.shape), spec((1, width, local), lambda i: (i, 0, 0))],
        out_specs=spec((1, rows, local), lambda i: (i, 0, 0)),
        out_shape=shaped((count, rows, local), half),
        compiler_params=params(28),
        cost_estimate=cost(9),
        name="project",
    )(mixed, w_qkv)


def attend_kernel(q_ref, k_ref, v_ref, qcode_ref, kcode_ref, w_ref, heads_ref, lse_ref, out_ref):
    heads = q_ref.shape[2] // HEAD_DIM
    for h in range(heads):
        cols = slice(h * HEAD_DIM, (h + 1) * HEAD_DIM)
        keys = jnp.concatenate([k_ref[0, :, cols], kcode_ref[...]], axis=1)
        query = jnp.concatenate([q_ref[0, :, cols], qcode_ref[...]], axis=1)
        scores = dot(keys, query, ((1,), (1,)))
        top = jnp.max(scores, axis=0, keepdims=True)
        expo = jnp.exp(scores - top)
        total = jnp.sum(expo, axis=0, keepdims=True)
        out = dot(v_ref[0, :, cols], expo.astype(half), ((0,), (0,)))
        heads_ref[:, cols] = (out / total).T.astype(half)
        lse_ref[0, h : h + 1, :] = top + jnp.log(total)
    out_ref[...] = jnp.dot(heads_ref[...], w_ref[...], preferred_element_type=f32).astype(half)


def attend_call(qkv, qcode, kcode, w_out, chunk, first, count):
    _, rows, local = qkv.shape
    width = w_out.shape[1]
    heads = local // HEAD_DIM
    return pl.pallas_call(
        attend_kernel,
        grid=(count,),
        in_specs=[
            spec((1, chunk, local), lambda i: (0, first + i, 0)),
            spec((1, rows, local), lambda i: (1, 0, 0)),
            spec((1, rows, local), lambda i: (2, 0, 0)),
            spec((chunk, HEAD_DIM), lambda i: (first + i, 0)),
            fixed((rows, HEAD_DIM)),
            held(w_out.shape),
        ],
        out_specs=[
            spec((chunk, local), lambda i: (i, 0)),
            spec((1, heads, chunk), lambda i: (i, 0, 0)),
            spec((chunk, width), lambda i: (i, 0)),
        ],
        out_shape=[
            shaped((count * chunk, local), half),
            shaped((count, heads, chunk), f32),
            shaped((count * chunk, width), half),
        ],
        compiler_params=params(32),
        cost_estimate=cost(2 + 3.3 * count),
        name="attend",
    )(qkv, qkv, qkv, qcode, kcode, w_out)


def attend_back_kernel(final, layout, q_ref, k_ref, v_ref, qcode_ref, kcode_ref, lse_ref, w_ref, *refs):
    chunk, local = q_ref.shape[1:]
    pieces, refs, d_heads_ref = refs[: sum(layout)], refs[sum(layout) : -1], refs[-1]
    heads = local // HEAD_DIM
    step = pl.program_id(0)
    factor = HEAD_DIM ** (-0.5)
    if final:
        dk_old, dv_old, dq_ref, dk_ref, dv_ref, dk_acc, dv_acc = refs
    else:
        dq_ref, dk_acc, dv_acc = refs

    @pl.when(step == 0)
    def _():
        dk_acc[...] = dk_old[...] if final else jnp.zeros_like(dk_acc)
        dv_acc[...] = dv_old[...] if final else jnp.zeros_like(dv_acc)

    for d, count in enumerate(layout):

        @pl.when(step == d)
        def _(refs=pieces[sum(layout[:d]) :][:count]):
            at = 0
            for ref in refs:
                d_heads_ref[at : at + ref.shape[0], :] = dot(ref[...], w_ref[...], ((1,), (1,))).astype(half)
                at += ref.shape[0]

    for h in range(heads):
        cols = slice(h * HEAD_DIM, (h + 1) * HEAD_DIM)
        keys = jnp.concatenate([k_ref[0, :, cols], kcode_ref[...]], axis=1)
        query = jnp.concatenate([q_ref[0, :, cols], qcode_ref[...]], axis=1)
        grad = d_heads_ref[:, cols]
        scores = dot(keys, query, ((1,), (1,)))
        probs = jnp.exp(scores - lse_ref[0, h : h + 1, :])
        d_probs = dot(v_ref[0, :, cols], grad, ((1,), (1,)))
        inner = jnp.sum(probs * d_probs, axis=0, keepdims=True)
        d_scores = (probs * (d_probs - inner)).astype(half)
        dv_acc[:, cols] += dot(probs.astype(half), grad, ((1,), (0,)))
        dk_acc[:, cols] += dot(d_scores, q_ref[0, :, cols], ((1,), (0,)))
        dq = dot(k_ref[0, :, cols], d_scores, ((0,), (0,)))
        dq_ref[:, cols] = (dq.T * factor).astype(half)

    if final:

        @pl.when(step == pl.num_programs(0) - 1)
        def _():
            dk_ref[...] = dk_acc[...].astype(half)
            dv_ref[...] = dv_acc[...].astype(half)


def attend_back_call(qkv, qcode, kcode, lse, w_out, d_attn, first, sums):
    _, rows, local = qkv.shape
    _, heads, chunk = lse.shape
    count = len(d_attn)
    final = sums is not None
    whole = (rows, local)
    return pl.pallas_call(
        lambda *refs: attend_back_kernel(final, [len(pieces) for pieces in d_attn], *refs),
        grid=(count,),
        in_specs=[
            spec((1, chunk, local), lambda i: (0, first + i, 0)),
            spec((1, rows, local), lambda i: (1, 0, 0)),
            spec((1, rows, local), lambda i: (2, 0, 0)),
            spec((chunk, HEAD_DIM), lambda i: (first + i, 0)),
            fixed((rows, HEAD_DIM)),
            spec((1, heads, chunk), lambda i: (first + i, 0, 0)),
            held(w_out.shape),
        ]
        + [held(piece.shape) for piece in flat(d_attn)]
        + ([held(whole)] * 2 if final else []),
        out_specs=[spec((chunk, local), lambda i: (i, 0))] + [fixed(whole)] * 2,
        out_shape=[shaped((count * chunk, local), half)] + [shaped(whole, half if final else f32)] * 2,
        scratch_shapes=([pltpu.VMEM(whole, f32)] * 2 if final else []) + [pltpu.VMEM((chunk, local), half)],
        compiler_params=params(36),
        cost_estimate=cost(0 if final else 130),
        name="attend_back",
    )(qkv, qkv, qkv, qcode, kcode, lse, w_out, *flat(d_attn), *(sums if final else []))


def project_back_kernel(q_ref, k_ref, v_ref, w_ref, out_ref):
    total = None
    for i, ref in enumerate((q_ref, k_ref, v_ref)):
        part = dot(ref[...], w_ref[i], ((1,), (1,)))
        total = part if total is None else total + part
    out_ref[...] = total.astype(half)


def project_back_call(d_query, d_key, d_value, w_qkv, chunk, first, count, first_query):
    _, width, local = w_qkv.shape
    there = lambda i: (first + i, 0)
    return pl.pallas_call(
        project_back_kernel,
        grid=(count,),
        in_specs=[
            spec((chunk, local), lambda i: (first - first_query + i, 0)),
            spec((chunk, local), there),
            spec((chunk, local), there),
            held(w_qkv.shape),
        ],
        out_specs=spec((chunk, width), lambda i: (i, 0)),
        out_shape=shaped((count * chunk, width), half),
        compiler_params=params(32),
        cost_estimate=cost(0),
        name="project_back",
    )(d_query, d_key, d_value, w_qkv)


def total_of(terms):
    return jnp.sum(terms, axis=0, keepdims=True)


def mlp_kernel(count, *refs):
    x_refs = refs[:count]
    up_ref, b_ref, d_ref = refs[count : count + 3]
    hidden_ref, d_pre_ref, dx_ref, b_sum_ref, acc_ref = refs[-5:]
    step = pl.program_id(0)
    mixed = jnp.concatenate([ref[...] for ref in x_refs], axis=0) if count > 1 else x_refs[0][...]
    pre = jnp.dot(mixed, up_ref[...], preferred_element_type=f32) + b_ref[...]
    cumul = 0.5 * (1.0 + lax.erf(pre * 0.7071067811865476))
    density = jnp.exp(-0.5 * pre * pre) * 0.3989422804014327
    hidden_ref[...] = (pre * cumul).astype(half)
    d_pre = (d_ref[...].astype(f32) * (cumul + pre * density)).astype(half)
    d_pre_ref[...] = d_pre
    b_sum_ref[...] = total_of(d_pre.astype(f32))
    part = dot(d_pre, up_ref[...], ((1,), (1,)))

    @pl.when(step == 0)
    def _():
        acc_ref[...] = part

    @pl.when(step > 0)
    def _():
        acc_ref[...] += part

    @pl.when(step == pl.num_programs(0) - 1)
    def _():
        dx_ref[...] = acc_ref[...].astype(half)


def mlp_call(pieces, w_up, b_up, d_hidden, chunk, before):
    rows = sum(piece.shape[0] for piece in pieces)
    width, ff = w_up.shape
    block = min(1024, ff)
    here = lambda j: (chunk, j)
    operands = [*pieces, w_up, b_up[None, :], d_hidden]
    in_specs = [held(piece.shape) for piece in pieces] + [
        spec((width, block), lambda j: (0, j)),
        spec((1, block), lambda j: (0, j)),
        spec((rows, block), here),
    ]
    aliases = {}
    if before is not None:
        aliases = {len(operands): 0, len(operands) + 1: 1}
        operands += before
        in_specs += [pl.BlockSpec(memory_space=pl.ANY)] * 2
    return pl.pallas_call(
        lambda *refs: mlp_kernel(len(pieces), *refs),
        grid=(ff // block,),
        in_specs=in_specs,
        out_specs=[
            spec((rows, block), here),
            spec((rows, block), here),
            fixed((rows, width)),
            spec((1, block), lambda j: (0, j)),
        ],
        out_shape=[
            shaped((d_hidden.shape[0], ff), half),
            shaped((d_hidden.shape[0], ff), half),
            pltpu.VMEM((rows, width), half),
            shaped((1, ff), f32),
        ],
        scratch_shapes=[pltpu.VMEM((rows, width), f32)],
        input_output_aliases=aliases,
        compiler_params=params(24),
        cost_estimate=cost(3),
        name="mlp",
    )(*operands)


def summed(refs):
    total = None
    for ref in refs:
        part = ref[...].astype(f32)
        total = part if total is None else total + part
    return total


def middle_kernel(parts, span, slot_ref, *refs):
    tok_ref, gate_ref, shift_ref, scale_ref, mixed_ref, attended_ref = refs
    slot = slot_ref[span]
    attended = summed(parts)
    attended_ref[...] = attended
    normed, _ = normalize(tok_ref[...].astype(f32) + row_of(gate_ref, slot) * attended)
    mixed_ref[...] = (normed * (1.0 + row_of(scale_ref, slot)) + row_of(shift_ref, slot)).astype(half)


def back_b_kernel(parts, span, slot_ref, *refs):
    tok_ref, grad_ref, attended_ref, gate_ref, scale_ref, d_attn_ref, d_middle_ref, sums_ref = refs
    slot = slot_ref[span]
    gate = row_of(gate_ref, slot)
    attended = attended_ref[...]
    normed, recip = normalize(tok_ref[...].astype(f32) + gate * attended)
    d_mixed = summed(parts)
    back = norm_back(d_mixed * (1.0 + row_of(scale_ref, slot)), normed, recip)
    d_middle = grad_ref[...].astype(f32) + back
    d_middle_ref[...] = d_middle
    d_attn_ref[...] = (d_middle * gate).astype(half)
    sums_ref[0, 0:1, :] = total_of(d_middle * attended)
    sums_ref[0, 1:2, :] = total_of(d_mixed)
    sums_ref[0, 2:3, :] = total_of(d_mixed * normed)


def back_a_kernel(parts, span, slot_ref, *refs):
    tok_ref, d_middle_ref, scale_ref, out_ref, sums_ref = refs
    slot = slot_ref[span]
    normed, recip = normalize(tok_ref[...].astype(f32))
    d_mixed = summed(parts)
    back = norm_back(d_mixed * (1.0 + row_of(scale_ref, slot)), normed, recip)
    out_ref[...] = (d_middle_ref[...] + back).astype(half)
    sums_ref[0, 0:1, :] = total_of(d_mixed)
    sums_ref[0, 1:2, :] = total_of(d_mixed * normed)


def result_kernel(parts, span, slot_ref, *refs):
    tok_ref, grad_ref, attended_ref, gate_a_ref, gate_b_ref, out_ref, sums_ref = refs
    slot = slot_ref[span]
    middle = tok_ref[...].astype(f32) + row_of(gate_a_ref, slot) * attended_ref[...]
    mlp_out = summed(parts)
    out_ref[...] = (middle + row_of(gate_b_ref, slot) * mlp_out).astype(half)
    sums_ref[0, 0:1, :] = total_of(grad_ref[...].astype(f32) * mlp_out)


def on_own(kernel, name, me, slots, parts, whole, own, modes, columns, outs, terms):
    width = whole[0].shape[1]
    spans = slots.shape[0]
    rows = spans * SPAN
    parts = [part if isinstance(part, tuple) else (part,) for part in parts]
    arrays = [*flat(parts), *own]

    def call(me_ref, slot_ref, *refs):
        ins = refs[: len(arrays) + len(whole)]
        mode_refs = refs[len(ins) : len(ins) + len(columns)]
        out_refs = refs[len(ins) + len(columns) :]
        for span in range(spans):

            def view(ref, count=1):
                at = span % (spans // count) * SPAN
                return ref.at[at : at + SPAN, :]

            given, at = [], 0
            for part in parts:
                count = len(part)
                given.append(view(ins[at + span // (spans // count)], count))
                at += count
            own_refs = [view(ref) for ref in ins[at : at + len(own)]]
            whole_refs = [view(ref) for ref in ins[at + len(own) :]]
            targets = [view(ref) for ref in out_refs[: len(outs)]]
            sums = [ref.at[span : span + 1] for ref in out_refs[len(outs) :]]
            kernel(given, span, slot_ref, *whole_refs, *own_refs, *mode_refs, *targets, *sums)

    return pl.pallas_call(
        call,
        grid_spec=pltpu.PrefetchScalarGridSpec(
            num_scalar_prefetch=2,
            grid=(1,),
            in_specs=[held(array.shape) for array in arrays]
            + [spec((rows, width), lambda i, m, s: (m[0], 0))] * len(whole)
            + mode_specs(modes, columns),
            out_specs=[fixed((rows, width))] * len(outs) + ([fixed((spans, terms, width))] if terms else []),
        ),
        out_shape=[shaped((rows, width), kind) for kind in outs]
        + ([shaped((spans, terms, width), f32)] if terms else []),
        compiler_params=params(24),
        cost_estimate=cost(0 if name in ("result", "back_a") else 5),
        name=name,
    )(me[None], slots, *arrays, *[in_hbm(array) for array in whole], *([modes] * len(columns)))


def unpack_kernel(sum_ref, qkv_ref, out_ref):
    step = pl.program_id(0)

    @pl.when(step < 3)
    def _():
        qkv_ref[0] = sum_ref[...].astype(f32)

    @pl.when(step == 3)
    def _():
        out_ref[...] = sum_ref[...].astype(f32).T


def unpack_call(sums, local):
    rows = sums.shape[0]
    return pl.pallas_call(
        unpack_kernel,
        grid=(4,),
        in_specs=[spec((rows, local), lambda i: (0, i))],
        out_specs=[
            spec((1, rows, local), lambda i: (jnp.minimum(i, 2), 0, 0)),
            fixed((local, rows)),
        ],
        out_shape=[pltpu.HBM((3, rows, local), f32), pltpu.HBM((local, rows), f32)],
        compiler_params=params(16),
        cost_estimate=cost(2),
        name="unpack",
    )(in_hbm(sums))


def make_body(n_wide, n_narrow):
    def body(
        tokens,
        cotangent,
        noise_emb,
        offsets,
        lengths,
        group_ids,
        group_table,
        w_qkv,
        w_out,
        w_up,
        b_up,
        w_down,
        w_mod,
        b_mod,
    ):
        tok_dev, width = tokens.shape
        slots = offsets.shape[1]
        local = w_qkv.shape[2]
        groups = group_table.shape[0]
        rows = tok_dev // n_narrow
        spans = rows // SPAN
        last = n_narrow - 1
        me = lax.axis_index("narrow")
        place = lax.axis_index("wide")
        order = me ^ jnp.arange(n_narrow, dtype=jnp.int32)

        starts = (order[:, None] * spans + jnp.arange(spans, dtype=jnp.int32)[None, :]).reshape(-1, 1) * SPAN
        inside = (starts >= offsets) & (starts < offsets + lengths)
        slot_hot = inside.astype(f32)
        slot_of = jnp.sum(inside * jnp.arange(slots, dtype=jnp.int32)[None, :], axis=1).astype(jnp.int32)
        slot_own = slot_of[:spans]
        lanes = jnp.arange(HEAD_DIM, dtype=jnp.int32)
        same = jnp.repeat(slot_of, SPAN)[:, None] == lanes[None, :]
        kcode = same.astype(half)
        qcode = jnp.where(same, 0.0, MASKED).astype(half)

        group_hot = (group_ids[0][:, None] == jnp.arange(groups, dtype=jnp.int32)[None, :]).astype(f32)
        cond = noise_emb + jnp.dot(group_hot, group_table, precision=highest)
        silu_low = jax.nn.silu(cond).astype(half)
        w_mod_t = w_mod.transpose(1, 0, 2)

        silu_all = lax.all_gather(jnp.concatenate([silu_low, silu_low], axis=0), "wide", axis=0)

        own_a = modes_call(silu_low, w_mod_t, b_mod, 0, 2)
        got_a = exchange([own_a] * n_narrow, n_narrow)
        own_b = modes_call(after(silu_low, own_a), w_mod_t, b_mod, 2, 4)
        modes_a = in_order(got_a, me, 2)
        mixed_a = by_chunk(mix_kernel, "mix_a", after(order, own_b), slot_of, tokens, modes_a, (0, 1))
        qkv = project_call(mixed_a, w_qkv, HEAD_DIM ** (-0.5))

        far = attend_call(qkv, qcode, kcode, w_out, rows, last, 1)
        via = collect_far(far[2], n_narrow)
        got_b = exchange([after(own_b, far[1])] * n_narrow, n_narrow)
        near = far
        if last > 1:
            near = attend_call(qkv, after(qcode, far[1], silu_all), kcode, w_out, rows, 1, last - 1)
        own = attend_call(qkv, after(qcode, near[1]), kcode, w_out, rows, 0, 1)
        modes = jnp.concatenate([modes_a, in_order([after(got, near[1]) for got in got_b], me, 2)], axis=0)
        in_turn = [own, near, far] if last > 1 else [own, far]
        heads_out = jnp.concatenate([outs[0] for outs in in_turn], axis=0)
        lse = jnp.concatenate([outs[1] for outs in in_turn], axis=0)
        sent = [near[2][(d - 1) * rows : d * rows] for d in range(1, last)]
        mid = rows // 2
        if n_narrow == 4:
            via_two, via_one = [after(got, own[1]) for got in via]
            second = hop(sent[0][mid:], 1, n_narrow)
            first = hop(sent[1][:mid], 2, n_narrow)
            merged = [
                (half_chunk.astype(f32) + got.astype(f32)).astype(half)
                for half_chunk, got in ((sent[0][:mid], via_two), (sent[1][mid:], via_one))
            ]
            attended_parts = [
                own[2],
                (hop(merged[0], 1, n_narrow), second),
                (first, hop(merged[1], 2, n_narrow)),
            ]
        else:
            attended_parts = exchange([own[2]] + sent + [far[2]], n_narrow)

        calls = [[(d, 0), (d, 1)] for d in range(n_narrow)]
        if n_narrow == 4:
            calls[1:3] = [[(1, 0), (2, 0)], [(1, 1), (2, 1)]]
        halves = flat(calls)
        block = rows // 2
        order_mlp = jnp.stack([2 * (me ^ d) + h for d, h in halves])
        slot_mlp = slot_of.reshape(2 * n_narrow, -1)[jnp.array([2 * d + h for d, h in halves])].reshape(-1)
        d_mlp = by_chunk(gate_kernel, "d_mlp", after(order_mlp, own[1]), slot_mlp, cotangent, modes, (5,))
        d_hidden = product(d_mlp, w_down, ((1,), (1,)), "d_hidden")
        mixed_own, attended = on_own(
            middle_kernel, "middle", me, after(slot_own, d_hidden), attended_parts, [tokens], [],
            modes, (2, 3, 4), [half, f32], 0,
        )
        pieces = {(0, h): mixed_own[h * block : (h + 1) * block] for h in range(2)}

        def send(half):
            for d in range(1, n_narrow if n_narrow != 4 else 3):
                pieces[d, half] = hop(pieces[0, half], d, n_narrow)

        send(0)
        pair, d_mixed, b_sums, due = None, {}, [], []
        for k, call in enumerate(calls):
            given = [pieces[half_chunk] for half_chunk in call] if k else [mixed_own]
            if k == 3 and n_narrow == 4:
                given = [pieces[half_chunk] for half_chunk in call]
            outs = mlp_call(given, w_up, after(b_up, *due), d_hidden, k, pair)
            pair = list(outs[:2])
            for i, half_chunk in enumerate(call):
                d_mixed[half_chunk] = outs[2][i * block : (i + 1) * block] if call[0][0] != call[1][0] else outs[2]
            b_sums.append(outs[3])
            due = [outs[3]]
            if k == 1 and n_narrow == 4:
                pieces[3, 0] = hop(after(pieces[2, 0], outs[3]), 1, n_narrow)
                pieces[3, 1] = hop(after(pieces[1, 1], outs[3]), 2, n_narrow)
            if not k:
                pieces[0, 1] = after(pieces[0, 1], outs[3])
                send(1)
        hidden, d_pre = pair

        def of_distance(d):
            first, second = d_mixed[d, 0], d_mixed[d, 1]
            if first is second:
                return first
            return after(joined([first, second]), pieces[last, 0], pieces[last, 1])

        d_mixed_parts = exchange([of_distance(d) for d in range(n_narrow)], n_narrow)
        mixed_b = jnp.concatenate([mixed_own] + [pieces[half_chunk] for half_chunk in halves[2:]], axis=0)

        def mlp_chunks(array):
            at = {half_chunk: k * block for k, half_chunk in enumerate(halves)}
            return [
                joined([array[at[d, h] : at[d, h] + block] for h in range(2)]) for d in range(n_narrow)
            ]

        grad_b_up = after(sum(b_sums)[0], hidden)

        grad_w_up = product(mixed_b, d_pre, ((0,), (0,)), "grad_w_up", out=pltpu.HBM, micros=4)
        sum_w_up = lax.psum_scatter(grad_w_up, "wide", scatter_dimension=0, tiled=True)
        grad_w_down = product(
            d_mlp, hidden, ((0,), (0,)), "grad_w_down", out=pltpu.HBM, micros=4, gate=after(order, grad_w_up)
        )

        d_attn_own, d_middle, sums_b = on_own(
            back_b_kernel, "back_b", me, after(slot_own, grad_w_down), d_mixed_parts, [tokens, cotangent],
            [attended], modes, (2, 4), [half, f32], 3,
        )

        def to_modes(sums):
            sent = [lax.dynamic_slice_in_dim(sums, (me ^ d) * local, local, 2) for d in range(n_narrow)]
            got = exchange(sent, n_narrow)
            modes_back = jnp.einsum("bs,bgv->gsv", slot_hot, jnp.concatenate(got, axis=0), precision=highest)
            return sent, modes_back.astype(half)

        d_attn_near = spread_near(d_attn_own, n_narrow)

        mlp_sent = product(hidden, w_down, ((1,), (0,)), "mlp_out", micros=200, gate=after(order, sums_b))
        d_attn_pieces = spread(d_attn_near, n_narrow, mlp_sent)
        mlp_sent = after(mlp_sent, *d_attn_near[1:])
        mlp_parts = exchange(mlp_chunks(mlp_sent), n_narrow)
        back = attend_back_call(qkv, qcode, kcode, lse, w_out, d_attn_pieces[:last], 0, None)
        back_far = attend_back_call(
            qkv, after(qcode, back[0]), kcode, lse, w_out, d_attn_pieces[last:], last, back[1:]
        )
        d_key, d_value = back_far[1:]
        far_a = project_back_call(back_far[0], d_key, d_value, w_qkv, rows, last, 1, last)
        via_a = collect_far(far_a, n_narrow)
        near_a = project_back_call(back[0], after(d_key, far_a), d_value, w_qkv, rows, 0, last, 0)
        sent_a = [near_a[d * rows : (d + 1) * rows] for d in range(last)] + [far_a]
        near_sent = collect_near(sent_a, n_narrow, via_a)
        d_mixed_a_parts = exchange(sent_a[:1] + near_sent, n_narrow)
        sum_w_down = lax.psum_scatter(after(grad_w_down, *d_attn_near[1:]), "wide", scatter_dimension=0, tiled=True)

        d_query = jnp.concatenate([back[0], back_far[0]], axis=0)
        d_proj = jnp.concatenate([after(d_query, near_a), d_key, d_value], axis=1)
        wide_cols = d_proj.shape[1] + local
        grads = product(
            mixed_a, d_proj, ((0,), (0,)), "grad_w_qkv", block=local, out=pltpu.HBM, micros=0,
            columns=wide_cols, gate=after(order, *mlp_parts),
        )
        d_attn = jnp.concatenate([joined(pieces) for pieces in d_attn_pieces], axis=0)
        grads = product(
            d_attn, heads_out, ((0,), (0,)), "grad_w_out", block=local, out=pltpu.HBM, micros=0,
            columns=wide_cols, first=d_proj.shape[1], before=grads, gate=after(order, *via_a),
        )
        sum_rest = lax.psum_scatter(grads, "wide", scatter_dimension=0, tiled=True)
        result_own, sums_out = on_own(
            result_kernel, "result", me, after(slot_own, grads, *near_sent), mlp_parts, [tokens, cotangent],
            [attended], modes, (2, 5), [half], 1,
        )
        grad_tok_own, sums_a = on_own(
            back_a_kernel, "back_a", me, after(slot_own, result_own, sum_w_up), d_mixed_a_parts, [tokens],
            [d_middle], modes, (1,), [half], 2,
        )
        sums_sent, d_modes = to_modes(jnp.concatenate([sums_a, sums_b, sums_out], axis=1))
        d_silu_part = silu_back_call(after(d_modes, sum_w_down), w_mod_t).astype(half)
        d_silu = sum(part.astype(f32) for part in exchange([d_silu_part] * n_narrow, n_narrow))
        sigma = jax.nn.sigmoid(cond)
        grad_noise = d_silu * sigma * (1.0 + cond * (1.0 - sigma))
        table_part = jnp.dot(group_hot.T, grad_noise, precision=highest).astype(half)

        grad_tok_near = spread_near(after(grad_tok_own, d_silu_part), n_narrow)
        result_near = spread_near(after(result_own, d_silu_part), n_narrow)
        ff = w_up.shape[1]
        small = jnp.pad(grad_b_up.astype(half), (0, -ff % width)).reshape(-1, width)
        late = lax.all_gather(
            jnp.concatenate([d_modes.reshape(-1, width), small, table_part], axis=0), "wide", axis=0
        )
        result = settle(spread(result_near, n_narrow, late), after(order, sum_w_down))
        grad_tokens = settle(spread(grad_tok_near, n_narrow, late), after(order, result))

        col = width // n_wide
        ff_part = ff // n_wide
        part_b = local // n_wide
        silu_cols = lax.dynamic_slice_in_dim(silu_all[:, :slots], place * col, col, 2).reshape(-1, col)
        mode_rows = 6 * slots * local // width
        small_rows = mode_rows + small.shape[0]
        b_up_all = late[:, mode_rows:small_rows].reshape(n_wide, -1)[:, :ff]
        sum_b_up = jnp.sum(
            lax.dynamic_slice_in_dim(b_up_all, place * ff_part, ff_part, 1).astype(f32), axis=0
        )
        d_modes_all = late[:, :mode_rows].reshape(n_wide, 6, slots, local)
        d_modes_all = d_modes_all.transpose(1, 0, 2, 3).reshape(6, n_wide * slots, local)
        grad_w_mod = jnp.einsum("sd,gsv->gdv", silu_cols, d_modes_all, preferred_element_type=f32).transpose(1, 0, 2)
        sum_b_mod = jnp.sum(
            lax.dynamic_slice_in_dim(d_modes_all, place * part_b, part_b, 2).astype(f32), axis=1
        )
        sum_table = jnp.sum(
            lax.dynamic_slice_in_dim(late[:, small_rows:], place * col, col, 2).astype(f32), axis=0
        )

        out_qkv, out_w_out = unpack_call(after(sum_rest, result, grad_tokens), local)
        return (
            result,
            grad_tokens,
            grad_noise,
            sum_table,
            out_qkv,
            out_w_out,
            sum_w_up.astype(f32),
            sum_b_up,
            sum_w_down.astype(f32).T,
            grad_w_mod,
            sum_b_mod,
        )

    return body


def solution(mesh):
    in_specs = (
        P("wide", None),
        P("wide", None),
        P("wide", None),
        P("wide", None),
        P("wide", None),
        P("wide", None),
        P(),
        P(None, None, "narrow"),
        P("narrow", None),
        P(None, "narrow"),
        P("narrow"),
        P("narrow", None),
        P(None, None, "narrow"),
        P(None, "narrow"),
    )
    out_specs = (
        P("wide", None),
        P("wide", None),
        P("wide", None),
        P(None, "wide"),
        P(None, "wide", "narrow"),
        P("narrow", "wide"),
        P("wide", "narrow"),
        P(("narrow", "wide")),
        P("narrow", "wide"),
        P("wide", None, "narrow"),
        P(None, ("narrow", "wide")),
    )
    body = make_body(mesh.shape["wide"], mesh.shape["narrow"])
    return jax.shard_map(body, mesh=mesh, in_specs=in_specs, out_specs=out_specs, check_vma=False)
```

profile of v0, /device:TPU:0, one launch (start us, length us, event | category | flops | bytes accessed | tf_op | source)
XLA Modules:
  0.0 442.0 jit_solution(1791253375675906129)
XLA Ops:
  20.1 4.8 %modes.3 = f32[4,16,512]{2,1,0:T(8,128)} custom-call(bf16[16,2048]{1,0:T(8,128)(2,1)S(1)} %get-tuple-element.99.silu_ref, bf16[6,2048,512]{2,1,0:T(8,128)(2,1)} %bitcast.60, f32[6,1,512]{2,1,0:T(1,128)S(1)} %broadcast_in_dim.41.b_ref), custom_call_target="tpu_custom_call" | custom-call | flops 6899999744 | tf_op jit(solution)/shard_map/modes/pallas_call | solution.py:162
  32.9 7.0 %project.1.q_ref.k_ref.v_ref.refs_0_.refs_1_.refs_2_ = bf16[3,1024,512]{2,1,0:T(8,128)(2,1)S(1)} custom-call(bf16[1024,2048]{1,0:T(8,128)(2,1)S(1)} %mix_a.1.refs_0_.left_ref, bf16[3,2048,512]{2,1,0:T(8,128)(2,1)S(1)} %bitcast.46), custom_call_target="tpu_custom_call" | custom-call | flops 10350000128 | tf_op jit(solution)/shard_map/project/pallas_call | solution.py:285
  54.0 7.0 %attend.4 = (bf16[512,512]{1,0:T(8,128)(2,1)S(1)}, f32[2,4,256]{2,1,0:T(4,128)S(1)}, bf16[512,2048]{1,0:T(8,128)(2,1)S(1)}) custom-call(bf16[3,1024,512]{2,1,0:T(8,128)(2,1)S(1)} %project.1.q_ref.k_ref.v_ref.refs_0_.refs_1_.refs_2_, bf16[3,1024,512]{2,1,0:T(8,128)(2,1)S(1)} %project.1.q_ref.k_ref.v_ref.refs_0_.refs_1_.refs_2_, ...), custom_call_target="tpu_custom_call" | custom-call | flops 9889999872 | tf_op jit(solution)/shard_map/attend/pallas_call | solution.py:317
  74.7 9.7 %d_hidden.1.refs_3_.refs_4_ = bf16[1024,2048]{1,0:T(8,128)(2,1)S(1)} custom-call(bf16[1024,2048]{1,0:T(8,128)(2,1)S(1)} %d_mlp.1.left_ref, bf16[2048,2048]{1,0:T(8,128)(2,1)S(1)} %bitcast.58), custom_call_target="tpu_custom_call" | custom-call | flops 4600000000 | tf_op jit(solution)/shard_map/d_hidden/pallas_call | solution.py:269
  91.8 7.0 %mlp.4 = (bf16[1024,2048]{1,0:T(8,128)(2,1)S(1)}, bf16[1024,2048]{1,0:T(8,128)(2,1)S(1)}, bf16[256,2048]{1,0:T(8,128)(2,1)S(1)}, f32[1,2048]{1,0:T(1,128)S(1)}) custom-call(bf16[256,2048]{1,0:T(8,128)(2,1)S(1)} %get-tuple-element.118.refs_0_, bf16[2048,2048]{1,0:T(8,128)(2,1)S(1)} %bitcast.44, f32[1,2048]{1,0:T(1,128)S(1)} %bitcast.49, ...), custom_call_target="tpu_custom_call" | custom-call | flops 3449999872 | tf_op jit(solution)/shard_map/mlp/pallas_call | solution.py:497
  106.0 7.2 %mlp.5 = (bf16[1024,2048]{1,0:T(8,128)(2,1)S(1)}, bf16[1024,2048]{1,0:T(8,128)(2,1)S(1)}, bf16[256,2048]{1,0:T(8,128)(2,1)S(1)}, f32[1,2048]{1,0:T(1,128)S(1)}) custom-call(bf16[128,2048]{1,0:T(8,128)(2,1)S(1)} %collective-permute-done.13.refs_0_, ...), custom_call_target="tpu_custom_call", output_to_operand_aliasing={{0}: (5, {}), {1}: (6, {})} | custom-call | flops 3449999872 | tf_op jit(solution)/shard_map/mlp/pallas_call | solution.py:497
  116.6 7.0 %mlp.6 = (bf16[1024,2048]{1,0:T(8,128)(2,1)S(1)}, bf16[1024,2048]{1,0:T(8,128)(2,1)S(1)}, bf16[256,2048]{1,0:T(8,128)(2,1)S(1)}, f32[1,2048]{1,0:T(1,128)S(1)}) custom-call(bf16[128,2048]{1,0:T(8,128)(2,1)S(1)} %collective-permute-done.15.refs_0_, ...), custom_call_target="tpu_custom_call", output_to_operand_aliasing={{0}: (5, {}), {1}: (6, {})} | custom-call | flops 3449999872 | tf_op jit(solution)/shard_map/mlp/pallas_call | solution.py:497
  128.9 8.0 %mlp.7 = (bf16[1024,2048]{1,0:T(8,128)(2,1)S(1)}, bf16[1024,2048]{1,0:T(8,128)(2,1)S(1)}, bf16[256,2048]{1,0:T(8,128)(2,1)}, f32[1,2048]{1,0:T(1,128)S(1)}) custom-call(bf16[128,2048]{1,0:T(8,128)(2,1)S(1)} %collective-permute-done.14.refs_0_, bf16[128,2048]{1,0:T(8,128)(2,1)S(1)} %collective-permute-done.16.refs_1_, ...), custom_call_target="tpu_custom_call", output_to_operand_aliasing={{0}: (5, {}), {1}: (6, {})} | custom-call | flops 3449999872 | tf_op jit(solution)/shard_map/mlp/pallas_call | solution.py:497
  139.9 11.7 %grad_w_up.1 = bf16[2048,2048]{1,0:T(8,128)(2,1)} custom-call(bf16[1024,2048]{1,0:T(8,128)(2,1)S(1)} %constant_dynamic-update-slice_fusion.left_ref, bf16[1024,2048]{1,0:T(8,128)(2,1)S(1)} %get-tuple-element.135.right_ref), custom_call_target="tpu_custom_call" | custom-call | flops 4600000000 | tf_op jit(solution)/shard_map/grad_w_up/pallas_call | solution.py:269
  156.1 11.3 %grad_w_down.1 = bf16[2048,2048]{1,0:T(8,128)(2,1)} custom-call(bf16[1024,2048]{1,0:T(8,128)(2,1)S(1)} %copy-done.46, bf16[1024,2048]{1,0:T(8,128)(2,1)S(1)} %copy-done.3, s32[4]{0:T(128)S(1)} %get-tuple-element.179.order_ref.refs_0_.refs_1_), custom_call_target="tpu_custom_call" | custom-call | flops 4600000000 | tf_op jit(solution)/shard_map/grad_w_down/pallas_call | solution.py:269
  167.4 4.8 %collective-permute-done.19.refs_2_ = bf16[256,2048]{1,0:T(8,128)(2,1)} collective-permute-done((bf16[256,2048]{1,0:T(8,128)(2,1)}, bf16[256,2048]{1,0:T(8,128)(2,1)}, u32[]{:S(2)}, u32[]{:S(2)}) %collective-permute-start.19) | collective-permute-done | bytes 1048608 | tf_op jit(solution)/shard_map/ppermute | solution.py:69
  173.9 7.4 %back_b.1 = (bf16[256,2048]{1,0:T(8,128)(2,1)}, f32[256,2048]{1,0:T(8,128)S(1)}, f32[4,3,2048]{2,1,0:T(4,128)S(1)}) custom-call(s32[1]{0:T(128)} %bitcast.13.me_ref, s32[4]{0:T(128)S(1)} %bitcast.54, bf16[256,2048]{1,0:T(8,128)(2,1)S(1)} %copy-done.44, bf16[256,2048]{1,0:T(8,128)(2,1)} %collective-permute-done.18.refs_1_, ...), custom_call_target="tpu_custom_call" | custom-call | flops 5750000128 | tf_op jit(solution)/shard_map/back_b/pallas_call | solution.py:602
  187.9 10.3 %mlp_out.1 = bf16[1024,2048]{1,0:T(8,128)(2,1)S(1)} custom-call(bf16[1024,2048]{1,0:T(8,128)(2,1)S(1)} %copy-done.4, bf16[2048,2048]{1,0:T(8,128)(2,1)S(1)} %copy-done.38, s32[4]{0:T(128)S(1)} %get-tuple-element.179.order_ref.refs_0_.refs_1_), custom_call_target="tpu_custom_call" | custom-call | flops 230000001024 | tf_op jit(solution)/shard_map/mlp_out/pallas_call | solution.py:269
  220.9 15.3 %attend_back.2 = (bf16[768,512]{1,0:T(8,128)(2,1)S(1)}, f32[1024,512]{1,0:T(8,128)S(1)}, f32[1024,512]{1,0:T(8,128)S(1)}) custom-call(bf16[3,1024,512]{2,1,0:T(8,128)(2,1)S(1)} %copy-done.6, bf16[3,1024,512]{2,1,0:T(8,128)(2,1)S(1)} %copy-done.6, bf16[3,1024,512]{2,1,0:T(8,128)(2,1)S(1)} %copy-done.6, bf16[1024,128]{1,0:T(8,128)(2,1)S(1)} %copy-done.30, ...), custom_call_target="tpu_custom_call" | custom-call | flops 149500002304 | tf_op jit(solution)/shard_map/attend_back/pallas_call | solution.py:398
  243.7 6.4 %attend_back.3 = (bf16[256,512]{1,0:T(8,128)(2,1)S(1)}, bf16[1024,512]{1,0:T(8,128)(2,1)S(1)}, bf16[1024,512]{1,0:T(8,128)(2,1)S(1)}) custom-call(bf16[3,1024,512]{2,1,0:T(8,128)(2,1)S(1)} %copy-done.6, bf16[3,1024,512]{2,1,0:T(8,128)(2,1)S(1)} %copy-done.6, bf16[3,1024,512]{2,1,0:T(8,128)(2,1)S(1)} %copy-done.6, bf16[1024,128]{1,0:T(8,128)(2,1)S(1)} %copy-done.30, ...), custom_call_target="tpu_custom_call" | custom-call | tf_op jit(solution)/shard_map/attend_back/pallas_call | solution.py:398
  253.3 5.7 %project_back.3 = bf16[768,2048]{1,0:T(8,128)(2,1)S(1)} custom-call(bf16[768,512]{1,0:T(8,128)(2,1)S(1)} %get-tuple-element.155.q_ref, bf16[1024,512]{1,0:T(8,128)(2,1)S(1)} %get-tuple-element.162.k_ref, bf16[1024,512]{1,0:T(8,128)(2,1)S(1)} %get-tuple-element.161.v_ref, bf16[3,2048,512]{2,1,0:T(8,128)(2,1)S(1)} %bitcast.48), custom_call_target="tpu_custom_call" | custom-call | tf_op jit(solution)/shard_map/project_back/pallas_call | solution.py:432
  264.9 6.4 %collective-permute-done.29 = bf16[128,2048]{1,0:T(8,128)(2,1)S(1)} collective-permute-done((bf16[128,2048]{1,0:T(8,128)(2,1)S(1)}, bf16[128,2048]{1,0:T(8,128)(2,1)S(1)}, u32[]{:S(2)}, u32[]{:S(2)}) %collective-permute-start.29) | collective-permute-done | bytes 524320 | tf_op jit(solution)/shard_map/ppermute | solution.py:69
  273.7 8.8 %grad_w_qkv.1.refs_0_ = bf16[2048,2048]{1,0:T(8,128)(2,1)} custom-call(bf16[1024,2048]{1,0:T(8,128)(2,1)S(1)} %copy-done.11, bf16[1024,1536]{1,0:T(8,128)(2,1)S(1)} %pad_maximum_fusion.right_ref, s32[4]{0:T(128)S(1)} %get-tuple-element.179.order_ref.refs_0_.refs_1_), custom_call_target="tpu_custom_call" | custom-call | tf_op jit(solution)/shard_map/grad_w_qkv/pallas_call | solution.py:269
  301.5 12.3 %collective-permute-done.30.refs_1_ = bf16[256,2048]{1,0:T(8,128)(2,1)} collective-permute-done((bf16[256,2048]{1,0:T(8,128)(2,1)}, bf16[256,2048]{1,0:T(8,128)(2,1)}, u32[]{:S(2)}, u32[]{:S(2)}) %collective-permute-start.30) | collective-permute-done | bytes 1048608 | tf_op jit(solution)/shard_map/ppermute | solution.py:69
  318.0 4.5 %back_a.1 = (bf16[256,2048]{1,0:T(8,128)(2,1)S(1)}, f32[4,2,2048]{2,1,0:T(2,128)S(1)}) custom-call(s32[1]{0:T(128)} %bitcast.13.me_ref, s32[4]{0:T(128)S(1)} %bitcast.56, bf16[256,2048]{1,0:T(8,128)(2,1)S(1)} %slice.164.refs_0_, bf16[256,2048]{1,0:T(8,128)(2,1)} %collective-permute-done.30.refs_1_, bf16[256,2048]{1,0:T(8,128)(2,1)} %collective-permute-done.31.refs_2_, ...), custom_call_target="tpu_custom_call" | custom-call | tf_op jit(solution)/shard_map/back_a/pallas_call | solution.py:602
  332.5 8.4 %silu_back.1 = f32[16,2048]{1,0:T(8,128)S(1)} custom-call(bf16[6,16,512]{2,1,0:T(8,128)(2,1)S(1)} %fusion.d_ref, bf16[6,2048,512]{2,1,0:T(8,128)(2,1)} %bitcast.61), custom_call_target="tpu_custom_call" | custom-call | tf_op jit(solution)/shard_map/silu_back/pallas_call | solution.py:193
  353.0 22.7 %all-gather.2 = bf16[8,28,2048]{2,1,0:T(8,128)(2,1)} all-gather(bf16[1,28,2048]{2,1,0:T(8,128)(2,1)S(1)} %maximum_bitcast_fusion), channel_id=3, replica_groups=mesh['wide'=8,'narrow'=4] {'wide'}, dimensions={0}, use_global_device_ids=true | all-gather | bytes 1032192 | tf_op jit(solution)/shard_map/all_gather | solution.py:854
  401.4 5.8 %collective-permute-done.40.refs_4_ = bf16[128,2048]{1,0:T(8,128)(2,1)} collective-permute-done((bf16[128,2048]{1,0:T(8,128)(2,1)}, bf16[128,2048]{1,0:T(8,128)(2,1)}, u32[]{:S(2)}, u32[]{:S(2)}) %collective-permute-start.40) | collective-permute-done | bytes 524320 | tf_op jit(solution)/shard_map/ppermute | solution.py:69
  419.6 11.5 %reduce-scatter.8.cloned.1.call-done.sum_ref = bf16[256,2048]{1,0:T(8,128)(2,1)} async-done(((bf16[2048,2048]{1,0:T(8,128)(2,1)}), bf16[256,2048]{1,0:T(8,128)(2,1)}) %reduce-scatter.8.cloned.1.call-update) | async-done | bytes 1048592 | tf_op jit(solution)/shard_map/reduce_scatter | solution.py:834
  (355 shorter events, 215.3 us)
Async XLA Ops:
  7.2 44.3 %all-gather.5.cloned.1.call-start = ((), (), s32[]{:S(2)}) async-start(), calls=%async_computation.6 | async-start | bytes 1179648 | tf_op jit(solution)/shard_map/all_gather | solution.py:692
  17.9 283.7 %reduce-scatter.6.cloned.1.call-start = ((), (), s32[]{:S(2)}) async-start(), calls=%async_computation.4 | async-start | bytes 9437184 | tf_op jit(solution)/shard_map/reduce_scatter | solution.py:787
  61.2 23.3 %collective-permute-start.9 = (bf16[128,2048]{1,0:T(8,128)(2,1)S(1)}, bf16[128,2048]{1,0:T(8,128)(2,1)S(1)}, u32[]{:S(2)}, u32[]{:S(2)}) collective-permute-start(bf16[128,2048]{1,0:T(8,128)(2,1)S(1)} %get-tuple-element.232), channel_id=1, source_target_pairs={{0,2},{1,3},{2,0},{3,1},{4,6},{5,7},{6,4},{7,5},{8,10},{9,11},{10,... | collective-permute-start | bytes 1572872 | tf_op jit(solution)/shard_map/ppermute | solution.py:69
  61.8 22.8 %collective-permute-start.8 = (bf16[128,2048]{1,0:T(8,128)(2,1)S(1)}, bf16[128,2048]{1,0:T(8,128)(2,1)S(1)}, u32[]{:S(2)}, u32[]{:S(2)}) collective-permute-start(bf16[128,2048]{1,0:T(8,128)(2,1)S(1)} %get-tuple-element.233), channel_id=1, source_target_pairs={{0,1},{1,0},{2,3},{3,2},{4,5},{5,4},{6,7},{7,6},{8,9},{9,8},{10,11... | collective-permute-start | bytes 1572872 | tf_op jit(solution)/shard_map/ppermute | solution.py:69
  126.4 41.1 %collective-permute-start.18 = (bf16[256,2048]{1,0:T(8,128)(2,1)}, bf16[256,2048]{1,0:T(8,128)(2,1)}, u32[]{:S(2)}, u32[]{:S(2)}) collective-permute-start(bf16[256,2048]{1,0:T(8,128)(2,1)} %pad_maximum_fusion.1), channel_id=1, source_target_pairs={{0,1},{1,0},{2,3},{3,2},{4,5},{5,4},{6,7},{7,6},{8,9},{9,8},{10,11... | collective-permute-start | bytes 3145736 | tf_op jit(solution)/shard_map/ppermute | solution.py:69
  127.5 44.8 %collective-permute-start.19 = (bf16[256,2048]{1,0:T(8,128)(2,1)}, bf16[256,2048]{1,0:T(8,128)(2,1)}, u32[]{:S(2)}, u32[]{:S(2)}) collective-permute-start(bf16[256,2048]{1,0:T(8,128)(2,1)} %pad_maximum_fusion.2), channel_id=1, source_target_pairs={{0,2},{1,3},{2,0},{3,1},{4,6},{5,7},{6,4},{7,5},{8,10},{9,11},{10,... | collective-permute-start | bytes 3145736 | tf_op jit(solution)/shard_map/ppermute | solution.py:69
  138.9 33.4 %collective-permute-start.20 = (bf16[256,2048]{1,0:T(8,128)(2,1)}, bf16[256,2048]{1,0:T(8,128)(2,1)}, u32[]{:S(2)}, u32[]{:S(2)}) collective-permute-start(bf16[256,2048]{1,0:T(8,128)(2,1)} %get-tuple-element.143), channel_id=1, source_target_pairs={{0,3},{1,2},{2,1},{3,0},{4,7},{5,6},{6,5},{7,4},{8,11},{9,10},{10,... | collective-permute-start | bytes 3145736 | tf_op jit(solution)/shard_map/ppermute | solution.py:69
  151.7 180.8 %reduce-scatter.4.cloned.1.call-start = ((), (), s32[]{:S(2)}) async-start(), calls=%async_computation.3 | async-start | bytes 9437184 | tf_op jit(solution)/shard_map/reduce_scatter | solution.py:820
  183.0 23.2 %collective-permute-start.21 = (bf16[256,2048]{1,0:T(8,128)(2,1)}, bf16[256,2048]{1,0:T(8,128)(2,1)}, u32[]{:S(2)}, u32[]{:S(2)}) collective-permute-start(bf16[256,2048]{1,0:T(8,128)(2,1)} %get-tuple-element.145.refs_7_), channel_id=1, source_target_pairs={{0,1},{1,0},{2,3},{3,2},{4,5},{5,4},{6,7},{7,6},{8,9},{9,8},{10,11... | collective-permute-start | bytes 3145736 | tf_op jit(solution)/shard_map/ppermute | solution.py:69
  204.4 35.7 %collective-permute-start.23 = (bf16[128,2048]{1,0:T(8,128)(2,1)}, bf16[128,2048]{1,0:T(8,128)(2,1)}, u32[]{:S(2)}, u32[]{:S(2)}) collective-permute-start(bf16[128,2048]{1,0:T(8,128)(2,1)} %slice.156), channel_id=1, source_target_pairs={{0,1},{1,0},{2,3},{3,2},{4,5},{5,4},{6,7},{7,6},{8,9},{9,8},{10,11... | collective-permute-start | bytes 1572872 | tf_op jit(solution)/shard_map/ppermute | solution.py:69
  208.1 32.0 %collective-permute-start.24 = (bf16[128,2048]{1,0:T(8,128)(2,1)}, bf16[128,2048]{1,0:T(8,128)(2,1)}, u32[]{:S(2)}, u32[]{:S(2)}) collective-permute-start(bf16[128,2048]{1,0:T(8,128)(2,1)} %slice.157), channel_id=1, source_target_pairs={{0,2},{1,3},{2,0},{3,1},{4,6},{5,7},{6,4},{7,5},{8,10},{9,11},{10,... | collective-permute-start | bytes 1572872 | tf_op jit(solution)/shard_map/ppermute | solution.py:69
  211.0 220.2 %reduce-scatter.8.cloned.1.call-start = ((), (), s32[]{:S(2)}) async-start(), calls=%async_computation.5 | async-start | bytes 9437184 | tf_op jit(solution)/shard_map/reduce_scatter | solution.py:834
  213.5 49.4 %collective-permute-start.25 = (bf16[256,2048]{1,0:T(8,128)(2,1)}, bf16[256,2048]{1,0:T(8,128)(2,1)}, u32[]{:S(2)}, u32[]{:S(2)}) collective-permute-start(bf16[256,2048]{1,0:T(8,128)(2,1)} %pad_maximum_fusion.5), channel_id=1, source_target_pairs={{0,1},{1,0},{2,3},{3,2},{4,5},{5,4},{6,7},{7,6},{8,9},{9,8},{10,11... | collective-permute-start | bytes 3145736 | tf_op jit(solution)/shard_map/ppermute | solution.py:69
  214.7 50.2 %collective-permute-start.26 = (bf16[256,2048]{1,0:T(8,128)(2,1)}, bf16[256,2048]{1,0:T(8,128)(2,1)}, u32[]{:S(2)}, u32[]{:S(2)}) collective-permute-start(bf16[256,2048]{1,0:T(8,128)(2,1)} %pad_maximum_fusion.6), channel_id=1, source_target_pairs={{0,2},{1,3},{2,0},{3,1},{4,6},{5,7},{6,4},{7,5},{8,10},{9,11},{10,... | collective-permute-start | bytes 3145736 | tf_op jit(solution)/shard_map/ppermute | solution.py:69
  217.2 47.7 %collective-permute-start.27 = (bf16[256,2048]{1,0:T(8,128)(2,1)}, bf16[256,2048]{1,0:T(8,128)(2,1)}, u32[]{:S(2)}, u32[]{:S(2)}) collective-permute-start(bf16[256,2048]{1,0:T(8,128)(2,1)} %get-tuple-element.220), channel_id=1, source_target_pairs={{0,3},{1,2},{2,1},{3,0},{4,7},{5,6},{6,5},{7,4},{8,11},{9,10},{10,... | collective-permute-start | bytes 3145736 | tf_op jit(solution)/shard_map/ppermute | solution.py:69
  252.1 21.5 %collective-permute-start.28 = (bf16[128,2048]{1,0:T(8,128)(2,1)S(1)}, bf16[128,2048]{1,0:T(8,128)(2,1)S(1)}, u32[]{:S(2)}, u32[]{:S(2)}) collective-permute-start(bf16[128,2048]{1,0:T(8,128)(2,1)S(1)} %get-tuple-element.235), channel_id=1, source_target_pairs={{0,2},{1,3},{2,0},{3,1},{4,6},{5,7},{6,4},{7,5},{8,10},{9,11},{10,... | collective-permute-start | bytes 1572872 | tf_op jit(solution)/shard_map/ppermute | solution.py:69
  290.6 23.3 %collective-permute-start.30 = (bf16[256,2048]{1,0:T(8,128)(2,1)}, bf16[256,2048]{1,0:T(8,128)(2,1)}, u32[]{:S(2)}, u32[]{:S(2)}) collective-permute-start(bf16[256,2048]{1,0:T(8,128)(2,1)} %pad_maximum_fusion.7), channel_id=1, source_target_pairs={{0,1},{1,0},{2,3},{3,2},{4,5},{5,4},{6,7},{7,6},{8,9},{9,8},{10,11... | collective-permute-start | bytes 3145736 | tf_op jit(solution)/shard_map/ppermute | solution.py:69
  292.8 23.6 %collective-permute-start.31 = (bf16[256,2048]{1,0:T(8,128)(2,1)}, bf16[256,2048]{1,0:T(8,128)(2,1)}, u32[]{:S(2)}, u32[]{:S(2)}) collective-permute-start(bf16[256,2048]{1,0:T(8,128)(2,1)} %pad_maximum_fusion.8), channel_id=1, source_target_pairs={{0,2},{1,3},{2,0},{3,1},{4,6},{5,7},{6,4},{7,5},{8,10},{9,11},{10,... | collective-permute-start | bytes 3145736 | tf_op jit(solution)/shard_map/ppermute | solution.py:69
  346.8 28.9 %collective-permute-start.36 = (bf16[256,2048]{1,0:T(8,128)(2,1)}, bf16[256,2048]{1,0:T(8,128)(2,1)S(1)}, u32[]{:S(2)}, u32[]{:S(2)}) collective-permute-start(bf16[256,2048]{1,0:T(8,128)(2,1)} %copy-done.39), channel_id=1, source_target_pairs={{0,2},{1,3},{2,0},{3,1},{4,6},{5,7},{6,4},{7,5},{8,10},{9,11},{10,... | collective-permute-start | bytes 3145736 | tf_op jit(solution)/shard_map/ppermute | solution.py:69
  348.0 29.7 %collective-permute-start.35 = (bf16[256,2048]{1,0:T(8,128)(2,1)}, bf16[256,2048]{1,0:T(8,128)(2,1)S(1)}, u32[]{:S(2)}, u32[]{:S(2)}) collective-permute-start(bf16[256,2048]{1,0:T(8,128)(2,1)} %copy-done.39), channel_id=1, source_target_pairs={{0,1},{1,0},{2,3},{3,2},{4,5},{5,4},{6,7},{7,6},{8,9},{9,8},{10,11... | collective-permute-start | bytes 3145736 | tf_op jit(solution)/shard_map/ppermute | solution.py:69
  349.4 49.3 %collective-permute-start.43 = (bf16[256,2048]{1,0:T(8,128)(2,1)}, bf16[256,2048]{1,0:T(8,128)(2,1)S(1)}, u32[]{:S(2)}, u32[]{:S(2)}) collective-permute-start(bf16[256,2048]{1,0:T(8,128)(2,1)} %copy-done.41), channel_id=1, source_target_pairs={{0,2},{1,3},{2,0},{3,1},{4,6},{5,7},{6,4},{7,5},{8,10},{9,11},{10,... | collective-permute-start | bytes 3145736 | tf_op jit(solution)/shard_map/ppermute | solution.py:69
  350.0 49.5 %collective-permute-start.42 = (bf16[256,2048]{1,0:T(8,128)(2,1)}, bf16[256,2048]{1,0:T(8,128)(2,1)}, u32[]{:S(2)}, u32[]{:S(2)}) collective-permute-start(bf16[256,2048]{1,0:T(8,128)(2,1)} %copy-done.41), channel_id=1, source_target_pairs={{0,1},{1,0},{2,3},{3,2},{4,5},{5,4},{6,7},{7,6},{8,9},{9,8},{10,11... | collective-permute-start | bytes 3145736 | tf_op jit(solution)/shard_map/ppermute | solution.py:69
  376.5 30.7 %collective-permute-start.40 = (bf16[128,2048]{1,0:T(8,128)(2,1)}, bf16[128,2048]{1,0:T(8,128)(2,1)}, u32[]{:S(2)}, u32[]{:S(2)}) collective-permute-start(bf16[128,2048]{1,0:T(8,128)(2,1)} %slice.165), channel_id=1, source_target_pairs={{0,1},{1,0},{2,3},{3,2},{4,5},{5,4},{6,7},{7,6},{8,9},{9,8},{10,11... | collective-permute-start | bytes 1572872 | tf_op jit(solution)/shard_map/ppermute | solution.py:69
  378.5 28.6 %collective-permute-start.41 = (bf16[128,2048]{1,0:T(8,128)(2,1)}, bf16[128,2048]{1,0:T(8,128)(2,1)}, u32[]{:S(2)}, u32[]{:S(2)}) collective-permute-start(bf16[128,2048]{1,0:T(8,128)(2,1)} %slice.166), channel_id=1, source_target_pairs={{0,2},{1,3},{2,0},{3,1},{4,6},{5,7},{6,4},{7,5},{8,10},{9,11},{10,... | collective-permute-start | bytes 1572872 | tf_op jit(solution)/shard_map/ppermute | solution.py:69
  (102 other events, 994.3 us)
Sparse Core Ops, SparseCore 0:
  18.0 23.7 all-gather.4
  151.8 90.3 reduce-scatter.5
  244.5 87.9 reduce-scatter.3
  334.7 96.4 reduce-scatter.7
where the time goes:
time: 450 us; the launch traced here: 442 us
  Pallas kernels  188 us (42%)
  local copies, waits for them, and re-layouts  68.6 us (15%)
  waiting for transfers between devices  65.1 us (14%)
  starting transfers between devices  52.6 us (12%)
  other arithmetic  23.5 us (5%)
  blocking collectives  22.7 us (5%)
  between operations  15.5 us (3%)
  matrix products  5.98 us (1%)
    pallas_call x6, Pallas kernels, product(): pl.pallas_call(lambda left_ref, right_ref, *refs: product_kernel(dims, No...  55.7 us
    ppermute x46, starting transfers between devices, hop(): lax.ppermute(values, 'narrow', [(i, i ^ distance) for i in range(size)])  52.4 us
    ppermute x46, waiting for transfers between devices, hop(): lax.ppermute(values, 'narrow', [(i, i ^ distance) for i in range(size)])  50.3 us
    unnamed x165, local copies, waits for them, and re-layouts  42.3 us
    pallas_call x4, Pallas kernels, mlp_call(): pl.pallas_call(lambda *refs: mlp_kernel(len(pieces), *refs), grid=(ff //...  29.3 us
    all_gather x1, blocking collectives, body(): lax.all_gather(jnp.concatenate([d_modes.reshape(-1, width), small, table_...  22.7 us
    pallas_call x2, Pallas kernels, attend_back_call(): pl.pallas_call(lambda *refs: attend_back_kernel(final, [len(pieces) for p...  21.6 us
    pallas_call x4, Pallas kernels, on_own(): pl.pallas_call(call, grid_spec=pltpu.PrefetchScalarGridSpec(num_scalar_pr...  19.5 us
  transfers between devices with their start and end apart: 50, of which 20 were waited for; matrix products, arithmetic and copies ran while one was open for 15% of the time, Pallas kernels for 40%

commit v1 on v0

--- a/solution.py
+++ b/solution.py
@@ -294,7 +294,13 @@
     )(mixed, w_qkv)
 
 
-def attend_kernel(q_ref, k_ref, v_ref, qcode_ref, kcode_ref, w_ref, heads_ref, lse_ref, out_ref):
+def attend_kernel(q_ref, k_ref, v_ref, qcode_ref, kcode_ref, w_all_ref, heads_ref, lse_ref, out_ref, w_ref, sem):
+    fetch = pltpu.make_async_copy(w_all_ref, w_ref, sem)
+
+    @pl.when(pl.program_id(0) == 0)
+    def _():
+        fetch.start()
+
     heads = q_ref.shape[2] // HEAD_DIM
     for h in range(heads):
         cols = slice(h * HEAD_DIM, (h + 1) * HEAD_DIM)
@@ -307,6 +313,11 @@
         out = dot(v_ref[0, :, cols], expo.astype(half), ((0,), (0,)))
         heads_ref[:, cols] = (out / total).T.astype(half)
         lse_ref[0, h : h + 1, :] = top + jnp.log(total)
+
+    @pl.when(pl.program_id(0) == 0)
+    def _():
+        fetch.wait()
+
     out_ref[...] = jnp.dot(heads_ref[...], w_ref[...], preferred_element_type=f32).astype(half)
 
 
@@ -323,7 +334,7 @@
             spec((1, rows, local), lambda i: (2, 0, 0)),
             spec((chunk, HEAD_DIM), lambda i: (first + i, 0)),
             fixed((rows, HEAD_DIM)),
-            held(w_out.shape),
+            pl.BlockSpec(memory_space=pl.ANY),
         ],
         out_specs=[
             spec((chunk, local), lambda i: (i, 0)),
@@ -335,10 +346,11 @@
             shaped((count, heads, chunk), f32),
             shaped((count * chunk, width), half),
         ],
+        scratch_shapes=[pltpu.VMEM(w_out.shape, half), pltpu.SemaphoreType.DMA],
         compiler_params=params(32),
         cost_estimate=cost(2 + 3.3 * count),
         name="attend",
-    )(qkv, qkv, qkv, qcode, kcode, w_out)
+    )(qkv, qkv, qkv, qcode, kcode, in_hbm(w_out))
 
 
 def attend_back_kernel(final, layout, q_ref, k_ref, v_ref, qcode_ref, kcode_ref, lse_ref, w_ref, *refs):

time: 450 us -> 450 us (level)
    unnamed x165 -> x161, local copies, waits for them, and re-layouts: 42.3 us -> 40.7 us
  transfers between devices with their start and end apart: 50 -> 50, of which waited for: 20 -> 20; matrix products, arithmetic and copies ran while one was open for 15% -> 15% of each run, Pallas kernels for 40% -> 41%
where the time goes in v1:
time: 450 us; the launch traced here: 442 us
  Pallas kernels  190 us (42%)
  local copies, waits for them, and re-layouts  67 us (15%)
  waiting for transfers between devices  65.2 us (14%)
  starting transfers between devices  52.6 us (12%)
  other arithmetic  23.5 us (5%)
  blocking collectives  22.7 us (5%)
  between operations  15.5 us (3%)
  matrix products  5.98 us (1%)
    pallas_call x6, Pallas kernels, product(): pl.pallas_call(lambda left_ref, right_ref, *refs: product_kernel(dims, No...  55.7 us
    ppermute x46, starting transfers between devices, hop(): lax.ppermute(values, 'narrow', [(i, i ^ distance) for i in range(size)])  52.4 us
    ppermute x46, waiting for transfers between devices, hop(): lax.ppermute(values, 'narrow', [(i, i ^ distance) for i in range(size)])  50.4 us
    unnamed x161, local copies, waits for them, and re-layouts  40.7 us
    pallas_call x4, Pallas kernels, mlp_call(): pl.pallas_call(lambda *refs: mlp_kernel(len(pieces), *refs), grid=(ff //...  29.2 us
    all_gather x1, blocking collectives, body(): lax.all_gather(jnp.concatenate([d_modes.reshape(-1, width), small, table_...  22.7 us
    pallas_call x2, Pallas kernels, attend_back_call(): pl.pallas_call(lambda *refs: attend_back_kernel(final, [len(pieces) for p...  21.6 us
    pallas_call x4, Pallas kernels, on_own(): pl.pallas_call(call, grid_spec=pltpu.PrefetchScalarGridSpec(num_scalar_pr...  19.5 us
  transfers between devices with their start and end apart: 50, of which 20 were waited for; matrix products, arithmetic and copies ran while one was open for 15% of the time, Pallas kernels for 41%

profile of v1, /device:TPU:0, one launch (start us, length us, event | category | flops | bytes accessed | tf_op | source)
XLA Modules:
  0.0 442.0 jit_solution(1121301121574937859)
XLA Ops:
  20.1 4.8 %modes.3 = f32[4,16,512]{2,1,0:T(8,128)} custom-call(bf16[16,2048]{1,0:T(8,128)(2,1)S(1)} %get-tuple-element.99.silu_ref, bf16[6,2048,512]{2,1,0:T(8,128)(2,1)} %bitcast.60, f32[6,1,512]{2,1,0:T(1,128)S(1)} %broadcast_in_dim.41.b_ref), custom_call_target="tpu_custom_call" | custom-call | flops 6899999744 | tf_op jit(solution)/shard_map/modes/pallas_call | solution.py:162
  32.8 7.0 %project.1.q_ref.k_ref.v_ref.refs_0_.refs_1_.refs_2_ = bf16[3,1024,512]{2,1,0:T(8,128)(2,1)S(1)} custom-call(bf16[1024,2048]{1,0:T(8,128)(2,1)S(1)} %mix_a.1.refs_0_.left_ref, bf16[3,2048,512]{2,1,0:T(8,128)(2,1)S(1)} %bitcast.46), custom_call_target="tpu_custom_call" | custom-call | flops 10350000128 | tf_op jit(solution)/shard_map/project/pallas_call | solution.py:285
  52.4 8.5 %attend.4 = (bf16[512,512]{1,0:T(8,128)(2,1)S(1)}, f32[2,4,256]{2,1,0:T(4,128)S(1)}, bf16[512,2048]{1,0:T(8,128)(2,1)S(1)}) custom-call(bf16[3,1024,512]{2,1,0:T(8,128)(2,1)S(1)} %project.1.q_ref.k_ref.v_ref.refs_0_.refs_1_.refs_2_, bf16[3,1024,512]{2,1,0:T(8,128)(2,1)S(1)} %project.1.q_ref.k_ref.v_ref.refs_0_.refs_1_.refs_2_, ...), custom_call_target="tpu_custom_call" | custom-call | flops 9889999872 | tf_op jit(solution)/shard_map/attend/pallas_call | solution.py:328
  74.6 9.7 %d_hidden.1.refs_3_.refs_4_ = bf16[1024,2048]{1,0:T(8,128)(2,1)S(1)} custom-call(bf16[1024,2048]{1,0:T(8,128)(2,1)S(1)} %d_mlp.1.left_ref, bf16[2048,2048]{1,0:T(8,128)(2,1)S(1)} %bitcast.58), custom_call_target="tpu_custom_call" | custom-call | flops 4600000000 | tf_op jit(solution)/shard_map/d_hidden/pallas_call | solution.py:269
  91.8 7.0 %mlp.4 = (bf16[1024,2048]{1,0:T(8,128)(2,1)S(1)}, bf16[1024,2048]{1,0:T(8,128)(2,1)S(1)}, bf16[256,2048]{1,0:T(8,128)(2,1)S(1)}, f32[1,2048]{1,0:T(1,128)S(1)}) custom-call(bf16[256,2048]{1,0:T(8,128)(2,1)S(1)} %get-tuple-element.118.refs_0_, bf16[2048,2048]{1,0:T(8,128)(2,1)S(1)} %bitcast.44, f32[1,2048]{1,0:T(1,128)S(1)} %bitcast.49, ...), custom_call_target="tpu_custom_call" | custom-call | flops 3449999872 | tf_op jit(solution)/shard_map/mlp/pallas_call | solution.py:509
  106.0 7.2 %mlp.5 = (bf16[1024,2048]{1,0:T(8,128)(2,1)S(1)}, bf16[1024,2048]{1,0:T(8,128)(2,1)S(1)}, bf16[256,2048]{1,0:T(8,128)(2,1)S(1)}, f32[1,2048]{1,0:T(1,128)S(1)}) custom-call(bf16[128,2048]{1,0:T(8,128)(2,1)S(1)} %collective-permute-done.13.refs_0_, ...), custom_call_target="tpu_custom_call", output_to_operand_aliasing={{0}: (5, {}), {1}: (6, {})} | custom-call | flops 3449999872 | tf_op jit(solution)/shard_map/mlp/pallas_call | solution.py:509
  116.5 7.0 %mlp.6 = (bf16[1024,2048]{1,0:T(8,128)(2,1)S(1)}, bf16[1024,2048]{1,0:T(8,128)(2,1)S(1)}, bf16[256,2048]{1,0:T(8,128)(2,1)S(1)}, f32[1,2048]{1,0:T(1,128)S(1)}) custom-call(bf16[128,2048]{1,0:T(8,128)(2,1)S(1)} %collective-permute-done.15.refs_0_, ...), custom_call_target="tpu_custom_call", output_to_operand_aliasing={{0}: (5, {}), {1}: (6, {})} | custom-call | flops 3449999872 | tf_op jit(solution)/shard_map/mlp/pallas_call | solution.py:509
  128.9 8.0 %mlp.7 = (bf16[1024,2048]{1,0:T(8,128)(2,1)S(1)}, bf16[1024,2048]{1,0:T(8,128)(2,1)S(1)}, bf16[256,2048]{1,0:T(8,128)(2,1)}, f32[1,2048]{1,0:T(1,128)S(1)}) custom-call(bf16[128,2048]{1,0:T(8,128)(2,1)S(1)} %collective-permute-done.14.refs_0_, bf16[128,2048]{1,0:T(8,128)(2,1)S(1)} %collective-permute-done.16.refs_1_, ...), custom_call_target="tpu_custom_call", output_to_operand_aliasing={{0}: (5, {}), {1}: (6, {})} | custom-call | flops 3449999872 | tf_op jit(solution)/shard_map/mlp/pallas_call | solution.py:509
  139.8 11.7 %grad_w_up.1 = bf16[2048,2048]{1,0:T(8,128)(2,1)} custom-call(bf16[1024,2048]{1,0:T(8,128)(2,1)S(1)} %constant_dynamic-update-slice_fusion.left_ref, bf16[1024,2048]{1,0:T(8,128)(2,1)S(1)} %get-tuple-element.135.right_ref), custom_call_target="tpu_custom_call" | custom-call | flops 4600000000 | tf_op jit(solution)/shard_map/grad_w_up/pallas_call | solution.py:269
  156.0 11.3 %grad_w_down.1 = bf16[2048,2048]{1,0:T(8,128)(2,1)} custom-call(bf16[1024,2048]{1,0:T(8,128)(2,1)S(1)} %copy-done.44, bf16[1024,2048]{1,0:T(8,128)(2,1)S(1)} %copy-done.3, s32[4]{0:T(128)S(1)} %get-tuple-element.179.order_ref.refs_0_.refs_1_), custom_call_target="tpu_custom_call" | custom-call | flops 4600000000 | tf_op jit(solution)/shard_map/grad_w_down/pallas_call | solution.py:269
  167.3 4.8 %collective-permute-done.19.refs_2_ = bf16[256,2048]{1,0:T(8,128)(2,1)} collective-permute-done((bf16[256,2048]{1,0:T(8,128)(2,1)}, bf16[256,2048]{1,0:T(8,128)(2,1)}, u32[]{:S(2)}, u32[]{:S(2)}) %collective-permute-start.19) | collective-permute-done | bytes 1048608 | tf_op jit(solution)/shard_map/ppermute | solution.py:69
  173.7 7.4 %back_b.1 = (bf16[256,2048]{1,0:T(8,128)(2,1)}, f32[256,2048]{1,0:T(8,128)S(1)}, f32[4,3,2048]{2,1,0:T(4,128)S(1)}) custom-call(s32[1]{0:T(128)} %bitcast.13.me_ref, s32[4]{0:T(128)S(1)} %bitcast.54, bf16[256,2048]{1,0:T(8,128)(2,1)S(1)} %copy-done.42, bf16[256,2048]{1,0:T(8,128)(2,1)} %collective-permute-done.18.refs_1_, ...), custom_call_target="tpu_custom_call" | custom-call | flops 5750000128 | tf_op jit(solution)/shard_map/back_b/pallas_call | solution.py:614
  187.7 10.3 %mlp_out.1 = bf16[1024,2048]{1,0:T(8,128)(2,1)S(1)} custom-call(bf16[1024,2048]{1,0:T(8,128)(2,1)S(1)} %copy-done.4, bf16[2048,2048]{1,0:T(8,128)(2,1)S(1)} %copy-done.36, s32[4]{0:T(128)S(1)} %get-tuple-element.179.order_ref.refs_0_.refs_1_), custom_call_target="tpu_custom_call" | custom-call | flops 230000001024 | tf_op jit(solution)/shard_map/mlp_out/pallas_call | solution.py:269
  220.8 15.2 %attend_back.2 = (bf16[768,512]{1,0:T(8,128)(2,1)S(1)}, f32[1024,512]{1,0:T(8,128)S(1)}, f32[1024,512]{1,0:T(8,128)S(1)}) custom-call(bf16[3,1024,512]{2,1,0:T(8,128)(2,1)S(1)} %copy-done.6, bf16[3,1024,512]{2,1,0:T(8,128)(2,1)S(1)} %copy-done.6, bf16[3,1024,512]{2,1,0:T(8,128)(2,1)S(1)} %copy-done.6, bf16[1024,128]{1,0:T(8,128)(2,1)S(1)} %copy-done.28, ...), custom_call_target="tpu_custom_call" | custom-call | flops 149500002304 | tf_op jit(solution)/shard_map/attend_back/pallas_call | solution.py:410
  243.6 6.4 %attend_back.3 = (bf16[256,512]{1,0:T(8,128)(2,1)S(1)}, bf16[1024,512]{1,0:T(8,128)(2,1)S(1)}, bf16[1024,512]{1,0:T(8,128)(2,1)S(1)}) custom-call(bf16[3,1024,512]{2,1,0:T(8,128)(2,1)S(1)} %copy-done.6, bf16[3,1024,512]{2,1,0:T(8,128)(2,1)S(1)} %copy-done.6, bf16[3,1024,512]{2,1,0:T(8,128)(2,1)S(1)} %copy-done.6, bf16[1024,128]{1,0:T(8,128)(2,1)S(1)} %copy-done.28, ...), custom_call_target="tpu_custom_call" | custom-call | tf_op jit(solution)/shard_map/attend_back/pallas_call | solution.py:410
  253.2 5.7 %project_back.3 = bf16[768,2048]{1,0:T(8,128)(2,1)S(1)} custom-call(bf16[768,512]{1,0:T(8,128)(2,1)S(1)} %get-tuple-element.155.q_ref, bf16[1024,512]{1,0:T(8,128)(2,1)S(1)} %get-tuple-element.162.k_ref, bf16[1024,512]{1,0:T(8,128)(2,1)S(1)} %get-tuple-element.161.v_ref, bf16[3,2048,512]{2,1,0:T(8,128)(2,1)S(1)} %bitcast.48), custom_call_target="tpu_custom_call" | custom-call | tf_op jit(solution)/shard_map/project_back/pallas_call | solution.py:444
  264.7 6.5 %collective-permute-done.29 = bf16[128,2048]{1,0:T(8,128)(2,1)S(1)} collective-permute-done((bf16[128,2048]{1,0:T(8,128)(2,1)S(1)}, bf16[128,2048]{1,0:T(8,128)(2,1)S(1)}, u32[]{:S(2)}, u32[]{:S(2)}) %collective-permute-start.29) | collective-permute-done | bytes 524320 | tf_op jit(solution)/shard_map/ppermute | solution.py:69
  273.6 8.8 %grad_w_qkv.1.refs_0_ = bf16[2048,2048]{1,0:T(8,128)(2,1)} custom-call(bf16[1024,2048]{1,0:T(8,128)(2,1)S(1)} %copy-done.11, bf16[1024,1536]{1,0:T(8,128)(2,1)S(1)} %pad_maximum_fusion.right_ref, s32[4]{0:T(128)S(1)} %get-tuple-element.179.order_ref.refs_0_.refs_1_), custom_call_target="tpu_custom_call" | custom-call | tf_op jit(solution)/shard_map/grad_w_qkv/pallas_call | solution.py:269
  301.4 12.4 %collective-permute-done.30.refs_1_ = bf16[256,2048]{1,0:T(8,128)(2,1)} collective-permute-done((bf16[256,2048]{1,0:T(8,128)(2,1)}, bf16[256,2048]{1,0:T(8,128)(2,1)}, u32[]{:S(2)}, u32[]{:S(2)}) %collective-permute-start.30) | collective-permute-done | bytes 1048608 | tf_op jit(solution)/shard_map/ppermute | solution.py:69
  317.9 4.5 %back_a.1 = (bf16[256,2048]{1,0:T(8,128)(2,1)S(1)}, f32[4,2,2048]{2,1,0:T(2,128)S(1)}) custom-call(s32[1]{0:T(128)} %bitcast.13.me_ref, s32[4]{0:T(128)S(1)} %bitcast.56, bf16[256,2048]{1,0:T(8,128)(2,1)S(1)} %slice.164.refs_0_, bf16[256,2048]{1,0:T(8,128)(2,1)} %collective-permute-done.30.refs_1_, bf16[256,2048]{1,0:T(8,128)(2,1)} %collective-permute-done.31.refs_2_, ...), custom_call_target="tpu_custom_call" | custom-call | tf_op jit(solution)/shard_map/back_a/pallas_call | solution.py:614
  332.5 8.4 %silu_back.1 = f32[16,2048]{1,0:T(8,128)S(1)} custom-call(bf16[6,16,512]{2,1,0:T(8,128)(2,1)S(1)} %fusion.d_ref, bf16[6,2048,512]{2,1,0:T(8,128)(2,1)} %bitcast.61), custom_call_target="tpu_custom_call" | custom-call | tf_op jit(solution)/shard_map/silu_back/pallas_call | solution.py:193
  353.0 22.7 %all-gather.2 = bf16[8,28,2048]{2,1,0:T(8,128)(2,1)} all-gather(bf16[1,28,2048]{2,1,0:T(8,128)(2,1)S(1)} %maximum_bitcast_fusion), channel_id=3, replica_groups=mesh['wide'=8,'narrow'=4] {'wide'}, dimensions={0}, use_global_device_ids=true | all-gather | bytes 1032192 | tf_op jit(solution)/shard_map/all_gather | solution.py:866
  401.4 5.8 %collective-permute-done.40.refs_4_ = bf16[128,2048]{1,0:T(8,128)(2,1)} collective-permute-done((bf16[128,2048]{1,0:T(8,128)(2,1)}, bf16[128,2048]{1,0:T(8,128)(2,1)}, u32[]{:S(2)}, u32[]{:S(2)}) %collective-permute-start.40) | collective-permute-done | bytes 524320 | tf_op jit(solution)/shard_map/ppermute | solution.py:69
  419.7 11.5 %reduce-scatter.8.cloned.1.call-done.sum_ref = bf16[256,2048]{1,0:T(8,128)(2,1)} async-done(((bf16[2048,2048]{1,0:T(8,128)(2,1)}), bf16[256,2048]{1,0:T(8,128)(2,1)}) %reduce-scatter.8.cloned.1.call-update) | async-done | bytes 1048592 | tf_op jit(solution)/shard_map/reduce_scatter | solution.py:846
  (351 shorter events, 213.7 us)
Async XLA Ops:
  7.2 44.3 %all-gather.5.cloned.1.call-start = ((), (), s32[]{:S(2)}) async-start(), calls=%async_computation.6 | async-start | bytes 1179648 | tf_op jit(solution)/shard_map/all_gather | solution.py:704
  17.9 283.5 %reduce-scatter.6.cloned.1.call-start = ((), (), s32[]{:S(2)}) async-start(), calls=%async_computation.4 | async-start | bytes 9437184 | tf_op jit(solution)/shard_map/reduce_scatter | solution.py:799
  61.1 23.4 %collective-permute-start.9 = (bf16[128,2048]{1,0:T(8,128)(2,1)S(1)}, bf16[128,2048]{1,0:T(8,128)(2,1)S(1)}, u32[]{:S(2)}, u32[]{:S(2)}) collective-permute-start(bf16[128,2048]{1,0:T(8,128)(2,1)S(1)} %get-tuple-element.232), channel_id=1, source_target_pairs={{0,2},{1,3},{2,0},{3,1},{4,6},{5,7},{6,4},{7,5},{8,10},{9,11},{10,... | collective-permute-start | bytes 1572872 | tf_op jit(solution)/shard_map/ppermute | solution.py:69
  61.7 22.8 %collective-permute-start.8 = (bf16[128,2048]{1,0:T(8,128)(2,1)S(1)}, bf16[128,2048]{1,0:T(8,128)(2,1)S(1)}, u32[]{:S(2)}, u32[]{:S(2)}) collective-permute-start(bf16[128,2048]{1,0:T(8,128)(2,1)S(1)} %get-tuple-element.233), channel_id=1, source_target_pairs={{0,1},{1,0},{2,3},{3,2},{4,5},{5,4},{6,7},{7,6},{8,9},{9,8},{10,11... | collective-permute-start | bytes 1572872 | tf_op jit(solution)/shard_map/ppermute | solution.py:69
  126.3 41.1 %collective-permute-start.18 = (bf16[256,2048]{1,0:T(8,128)(2,1)}, bf16[256,2048]{1,0:T(8,128)(2,1)}, u32[]{:S(2)}, u32[]{:S(2)}) collective-permute-start(bf16[256,2048]{1,0:T(8,128)(2,1)} %pad_maximum_fusion.1), channel_id=1, source_target_pairs={{0,1},{1,0},{2,3},{3,2},{4,5},{5,4},{6,7},{7,6},{8,9},{9,8},{10,11... | collective-permute-start | bytes 3145736 | tf_op jit(solution)/shard_map/ppermute | solution.py:69
  127.3 44.8 %collective-permute-start.19 = (bf16[256,2048]{1,0:T(8,128)(2,1)}, bf16[256,2048]{1,0:T(8,128)(2,1)}, u32[]{:S(2)}, u32[]{:S(2)}) collective-permute-start(bf16[256,2048]{1,0:T(8,128)(2,1)} %pad_maximum_fusion.2), channel_id=1, source_target_pairs={{0,2},{1,3},{2,0},{3,1},{4,6},{5,7},{6,4},{7,5},{8,10},{9,11},{10,... | collective-permute-start | bytes 3145736 | tf_op jit(solution)/shard_map/ppermute | solution.py:69
  138.9 33.2 %collective-permute-start.20 = (bf16[256,2048]{1,0:T(8,128)(2,1)}, bf16[256,2048]{1,0:T(8,128)(2,1)}, u32[]{:S(2)}, u32[]{:S(2)}) collective-permute-start(bf16[256,2048]{1,0:T(8,128)(2,1)} %get-tuple-element.143), channel_id=1, source_target_pairs={{0,3},{1,2},{2,1},{3,0},{4,7},{5,6},{6,5},{7,4},{8,11},{9,10},{10,... | collective-permute-start | bytes 3145736 | tf_op jit(solution)/shard_map/ppermute | solution.py:69
  151.6 180.9 %reduce-scatter.4.cloned.1.call-start = ((), (), s32[]{:S(2)}) async-start(), calls=%async_computation.3 | async-start | bytes 9437184 | tf_op jit(solution)/shard_map/reduce_scatter | solution.py:832
  182.8 23.3 %collective-permute-start.21 = (bf16[256,2048]{1,0:T(8,128)(2,1)}, bf16[256,2048]{1,0:T(8,128)(2,1)}, u32[]{:S(2)}, u32[]{:S(2)}) collective-permute-start(bf16[256,2048]{1,0:T(8,128)(2,1)} %get-tuple-element.145.refs_7_), channel_id=1, source_target_pairs={{0,1},{1,0},{2,3},{3,2},{4,5},{5,4},{6,7},{7,6},{8,9},{9,8},{10,11... | collective-permute-start | bytes 3145736 | tf_op jit(solution)/shard_map/ppermute | solution.py:69
  204.0 35.9 %collective-permute-start.23 = (bf16[128,2048]{1,0:T(8,128)(2,1)}, bf16[128,2048]{1,0:T(8,128)(2,1)}, u32[]{:S(2)}, u32[]{:S(2)}) collective-permute-start(bf16[128,2048]{1,0:T(8,128)(2,1)} %slice.156), channel_id=1, source_target_pairs={{0,1},{1,0},{2,3},{3,2},{4,5},{5,4},{6,7},{7,6},{8,9},{9,8},{10,11... | collective-permute-start | bytes 1572872 | tf_op jit(solution)/shard_map/ppermute | solution.py:69
  208.0 32.0 %collective-permute-start.24 = (bf16[128,2048]{1,0:T(8,128)(2,1)}, bf16[128,2048]{1,0:T(8,128)(2,1)}, u32[]{:S(2)}, u32[]{:S(2)}) collective-permute-start(bf16[128,2048]{1,0:T(8,128)(2,1)} %slice.157), channel_id=1, source_target_pairs={{0,2},{1,3},{2,0},{3,1},{4,6},{5,7},{6,4},{7,5},{8,10},{9,11},{10,... | collective-permute-start | bytes 1572872 | tf_op jit(solution)/shard_map/ppermute | solution.py:69
  210.9 220.3 %reduce-scatter.8.cloned.1.call-start = ((), (), s32[]{:S(2)}) async-start(), calls=%async_computation.5 | async-start | bytes 9437184 | tf_op jit(solution)/shard_map/reduce_scatter | solution.py:846
  213.4 49.4 %collective-permute-start.25 = (bf16[256,2048]{1,0:T(8,128)(2,1)}, bf16[256,2048]{1,0:T(8,128)(2,1)}, u32[]{:S(2)}, u32[]{:S(2)}) collective-permute-start(bf16[256,2048]{1,0:T(8,128)(2,1)} %pad_maximum_fusion.5), channel_id=1, source_target_pairs={{0,1},{1,0},{2,3},{3,2},{4,5},{5,4},{6,7},{7,6},{8,9},{9,8},{10,11... | collective-permute-start | bytes 3145736 | tf_op jit(solution)/shard_map/ppermute | solution.py:69
  214.6 50.1 %collective-permute-start.26 = (bf16[256,2048]{1,0:T(8,128)(2,1)}, bf16[256,2048]{1,0:T(8,128)(2,1)}, u32[]{:S(2)}, u32[]{:S(2)}) collective-permute-start(bf16[256,2048]{1,0:T(8,128)(2,1)} %pad_maximum_fusion.6), channel_id=1, source_target_pairs={{0,2},{1,3},{2,0},{3,1},{4,6},{5,7},{6,4},{7,5},{8,10},{9,11},{10,... | collective-permute-start | bytes 3145736 | tf_op jit(solution)/shard_map/ppermute | solution.py:69
  217.0 47.7 %collective-permute-start.27 = (bf16[256,2048]{1,0:T(8,128)(2,1)}, bf16[256,2048]{1,0:T(8,128)(2,1)}, u32[]{:S(2)}, u32[]{:S(2)}) collective-permute-start(bf16[256,2048]{1,0:T(8,128)(2,1)} %get-tuple-element.220), channel_id=1, source_target_pairs={{0,3},{1,2},{2,1},{3,0},{4,7},{5,6},{6,5},{7,4},{8,11},{9,10},{10,... | collective-permute-start | bytes 3145736 | tf_op jit(solution)/shard_map/ppermute | solution.py:69
  252.0 21.5 %collective-permute-start.28 = (bf16[128,2048]{1,0:T(8,128)(2,1)S(1)}, bf16[128,2048]{1,0:T(8,128)(2,1)S(1)}, u32[]{:S(2)}, u32[]{:S(2)}) collective-permute-start(bf16[128,2048]{1,0:T(8,128)(2,1)S(1)} %get-tuple-element.235), channel_id=1, source_target_pairs={{0,2},{1,3},{2,0},{3,1},{4,6},{5,7},{6,4},{7,5},{8,10},{9,11},{10,... | collective-permute-start | bytes 1572872 | tf_op jit(solution)/shard_map/ppermute | solution.py:69
  290.5 23.4 %collective-permute-start.30 = (bf16[256,2048]{1,0:T(8,128)(2,1)}, bf16[256,2048]{1,0:T(8,128)(2,1)}, u32[]{:S(2)}, u32[]{:S(2)}) collective-permute-start(bf16[256,2048]{1,0:T(8,128)(2,1)} %pad_maximum_fusion.7), channel_id=1, source_target_pairs={{0,1},{1,0},{2,3},{3,2},{4,5},{5,4},{6,7},{7,6},{8,9},{9,8},{10,11... | collective-permute-start | bytes 3145736 | tf_op jit(solution)/shard_map/ppermute | solution.py:69
  292.6 23.7 %collective-permute-start.31 = (bf16[256,2048]{1,0:T(8,128)(2,1)}, bf16[256,2048]{1,0:T(8,128)(2,1)}, u32[]{:S(2)}, u32[]{:S(2)}) collective-permute-start(bf16[256,2048]{1,0:T(8,128)(2,1)} %pad_maximum_fusion.8), channel_id=1, source_target_pairs={{0,2},{1,3},{2,0},{3,1},{4,6},{5,7},{6,4},{7,5},{8,10},{9,11},{10,... | collective-permute-start | bytes 3145736 | tf_op jit(solution)/shard_map/ppermute | solution.py:69
  346.8 28.8 %collective-permute-start.36 = (bf16[256,2048]{1,0:T(8,128)(2,1)}, bf16[256,2048]{1,0:T(8,128)(2,1)S(1)}, u32[]{:S(2)}, u32[]{:S(2)}) collective-permute-start(bf16[256,2048]{1,0:T(8,128)(2,1)} %copy-done.37), channel_id=1, source_target_pairs={{0,2},{1,3},{2,0},{3,1},{4,6},{5,7},{6,4},{7,5},{8,10},{9,11},{10,... | collective-permute-start | bytes 3145736 | tf_op jit(solution)/shard_map/ppermute | solution.py:69
  348.0 29.7 %collective-permute-start.35 = (bf16[256,2048]{1,0:T(8,128)(2,1)}, bf16[256,2048]{1,0:T(8,128)(2,1)S(1)}, u32[]{:S(2)}, u32[]{:S(2)}) collective-permute-start(bf16[256,2048]{1,0:T(8,128)(2,1)} %copy-done.37), channel_id=1, source_target_pairs={{0,1},{1,0},{2,3},{3,2},{4,5},{5,4},{6,7},{7,6},{8,9},{9,8},{10,11... | collective-permute-start | bytes 3145736 | tf_op jit(solution)/shard_map/ppermute | solution.py:69
  349.4 49.3 %collective-permute-start.43 = (bf16[256,2048]{1,0:T(8,128)(2,1)}, bf16[256,2048]{1,0:T(8,128)(2,1)S(1)}, u32[]{:S(2)}, u32[]{:S(2)}) collective-permute-start(bf16[256,2048]{1,0:T(8,128)(2,1)} %copy-done.39), channel_id=1, source_target_pairs={{0,2},{1,3},{2,0},{3,1},{4,6},{5,7},{6,4},{7,5},{8,10},{9,11},{10,... | collective-permute-start | bytes 3145736 | tf_op jit(solution)/shard_map/ppermute | solution.py:69
  350.0 49.5 %collective-permute-start.42 = (bf16[256,2048]{1,0:T(8,128)(2,1)}, bf16[256,2048]{1,0:T(8,128)(2,1)}, u32[]{:S(2)}, u32[]{:S(2)}) collective-permute-start(bf16[256,2048]{1,0:T(8,128)(2,1)} %copy-done.39), channel_id=1, source_target_pairs={{0,1},{1,0},{2,3},{3,2},{4,5},{5,4},{6,7},{7,6},{8,9},{9,8},{10,11... | collective-permute-start | bytes 3145736 | tf_op jit(solution)/shard_map/ppermute | solution.py:69
  376.5 30.7 %collective-permute-start.40 = (bf16[128,2048]{1,0:T(8,128)(2,1)}, bf16[128,2048]{1,0:T(8,128)(2,1)}, u32[]{:S(2)}, u32[]{:S(2)}) collective-permute-start(bf16[128,2048]{1,0:T(8,128)(2,1)} %slice.165), channel_id=1, source_target_pairs={{0,1},{1,0},{2,3},{3,2},{4,5},{5,4},{6,7},{7,6},{8,9},{9,8},{10,11... | collective-permute-start | bytes 1572872 | tf_op jit(solution)/shard_map/ppermute | solution.py:69
  378.5 28.7 %collective-permute-start.41 = (bf16[128,2048]{1,0:T(8,128)(2,1)}, bf16[128,2048]{1,0:T(8,128)(2,1)}, u32[]{:S(2)}, u32[]{:S(2)}) collective-permute-start(bf16[128,2048]{1,0:T(8,128)(2,1)} %slice.166), channel_id=1, source_target_pairs={{0,2},{1,3},{2,0},{3,1},{4,6},{5,7},{6,4},{7,5},{8,10},{9,11},{10,... | collective-permute-start | bytes 1572872 | tf_op jit(solution)/shard_map/ppermute | solution.py:69
  (100 other events, 985.2 us)
Sparse Core Ops, SparseCore 0:
  18.0 23.7 all-gather.4
  151.7 90.4 reduce-scatter.5
  244.5 87.9 reduce-scatter.3
  334.7 96.4 reduce-scatter.7
